TPU v7x, 128 devices: a whole 4x4x4 slice. The times are simulated.
128 devices in a mesh: bucket: 8 (over y, core), member: 16 (over z, x).
Axes of the slice: x: 4, y: 4, z: 4, core: 2. Of those that a mesh axis runs over, the one named last changes fastest.
Arguments:
- loader_rows: float32 [8192, 4096], P(('bucket', 'member')), may hold values from -12 to 12
- dest_bucket: int32 [8192], P(('bucket', 'member')), may hold values from 0 to 7, as said below
- dest_slot: int32 [8192], P(('bucket', 'member')), may hold values from 0 to 127, as said below
- noise: float32 [32768, 4096], P(('bucket', 'member')), may hold values from -12 to 12
Outputs:
- targets: float32 [32768, 4096], P(('bucket', 'member'))
Inputs may be any that keep to these rules, and one draw needn't show every extreme that they name: Loaded row r goes to bucket group dest_bucket[r] on the device of that group with the same member index as its loader device. No loader device sends more than 16 rows to one bucket group; on every member index one bucket group receives exactly 16 rows from every loader device, and every bucket group is so filled on some member index. `dest_slot`: rows that reach the same device have distinct slots.
All inputs are finite; a program needn't handle non-finite values.
Results may differ from a plain program's by a relative error of at most 0.012.
The roundings to bfloat16 on the way count: a program that leaves them out, or rounds other values in their place, can miss the bound.
Values may be sent and summed in bfloat16 or wider, within the bound.
A program may use at most 128 MiB of HBM per device.

v0:
```python
import math

import jax
import jax.numpy as jnp
from jax import lax
from jax.sharding import PartitionSpec as P

ROWS_DEV = 128
ITERS = 4


def tile_cost(panel, noise_rows, noise_norm, width):
    cross_term = lax.dot_general(
        panel, noise_rows, (((1,), (1,)), ((), ())), preferred_element_type=jnp.float32
    )
    panel_wide = panel.astype(jnp.float32)
    return (
        jnp.sum(panel_wide * panel_wide, axis=1)[:, None] + noise_norm[None, :] - 2.0 * cross_term
    ) / width


def body(loader_rows, dest_bucket, dest_slot, noise):
    groups = lax.axis_size("bucket")
    width = loader_rows.shape[1]
    noise_count = noise.shape[0]
    capacity = ROWS_DEV // groups
    epsilon = 0.64 / math.sqrt(width)
    rounded = loader_rows.astype(jnp.bfloat16)
    hits = (dest_bucket[:, None] == jnp.arange(groups, dtype=jnp.int32)[None, :]).astype(jnp.int32)
    ranks = jnp.sum((jnp.cumsum(hits, axis=0) - 1) * hits, axis=1)
    position = dest_bucket * capacity + ranks
    send_rows = jnp.zeros((groups * capacity, width), jnp.bfloat16).at[position].set(rounded)
    send_slots = jnp.full((groups * capacity,), ROWS_DEV, jnp.int32).at[position].set(dest_slot)
    got_rows, got_slots = (
        lax.all_to_all(send_rows, "bucket", split_axis=0, concat_axis=0, tiled=True),
        lax.all_to_all(send_slots, "bucket", split_axis=0, concat_axis=0, tiled=True),
    )
    data_rows = jnp.zeros((ROWS_DEV, width), jnp.bfloat16).at[got_slots].set(got_rows, mode="drop")
    live_rows = (
        jnp.zeros((ROWS_DEV,), jnp.bfloat16)
        .at[got_slots]
        .set(jnp.ones(got_slots.shape, jnp.bfloat16), mode="drop")
    )
    noise_rows = noise.astype(jnp.bfloat16)
    noise_wide = noise_rows.astype(jnp.float32)
    noise_norm = jnp.sum(noise_wide * noise_wide, axis=1)
    whole_rows, whole_live = (
        lax.all_gather(data_rows, "member", axis=0, tiled=True),
        lax.all_gather(live_rows, "member", axis=0, tiled=True),
    )
    cost_tile = tile_cost(whole_rows, noise_rows, noise_norm, width)
    alive_rows = whole_live > 0.5
    col_pot = jnp.zeros((noise_count,), jnp.float32)
    exponent = jnp.zeros(cost_tile.shape, jnp.float32)
    col_total = jnp.ones((noise_count,), jnp.float32)
    for sweep_index in range(ITERS):
        scores = (col_pot[None, :] - cost_tile) / epsilon
        local_peak = jnp.max(scores, axis=1)
        row_peak = lax.pmax(local_peak, "member")
        row_total = lax.psum(jnp.sum(jnp.exp(scores - row_peak[:, None]), axis=1), "member")
        row_pot = -epsilon * (row_peak + jnp.log(row_total))
        col_scores = (row_pot[:, None] - cost_tile) / epsilon
        col_peak = jnp.max(jnp.where(alive_rows[:, None], col_scores, -jnp.inf), axis=0)
        exponent = jnp.where(alive_rows[:, None], jnp.exp(col_scores - col_peak[None, :]), 0.0)
        col_total = jnp.sum(exponent, axis=0)
        col_pot = -epsilon * (col_peak + jnp.log(col_total))
    weights = (exponent / col_total[None, :]).astype(jnp.bfloat16)
    targets = lax.dot_general(
        weights, whole_rows, (((0,), (0,)), ((), ())), preferred_element_type=jnp.float32
    )
    return targets


def solution(mesh):
    return jax.shard_map(
        body,
        mesh=mesh,
        in_specs=(
            P(("bucket", "member"), None),
            P(("bucket", "member")),
            P(("bucket", "member")),
            P(("bucket", "member"), None),
        ),
        out_specs=P(("bucket", "member"), None),
        check_vma=False,
    )
```

profile of v0, /device:TPU:0, one launch (start us, length us, event | category | flops | bytes accessed | tf_op | source)
XLA Modules:
  0.0 500.2 jit_solution(14216818540153028822)
XLA Ops:
  6.5 0.7 fusion.20
  7.4 0.8 select_reduce_fusion.7
  8.9 0.9 scatter_custom_fusion
  10.5 4.6 all-to-all-start
  15.0 3.1 scatter_custom_fusion.2
  18.1 2.2 all-to-all-done
  20.3 3.6 all-to-all-start.1
  25.3 14.4 %all-to-all-done.1 = bf16[8,16,4096]{2,1,0:T(8,128)(2,1)S(1)} async-done(((bf16[8,16,4096]{2,1,0:T(8,128)(2,1)}), bf16[8,16,4096]{2,1,0:T(8,128)(2,1)S(1)}, u32[]{:S(2)}, u32[]{:S(2)}) %all-to-all-start.1) | async-done | bytes 1048608 | tf_op jit(solution)/shard_map/all_to_all | solution.py:35
  39.7 3.0 scatter_custom_fusion.3
  42.8 2.6 multiply_reduce_fusion.1
  45.3 1.3 scatter_custom_fusion.1
  46.7 21.9 %all-gather = bf16[16,1,128]{2,1,0:T(2,128)(2,1)S(1)} all-gather(bf16[1,1,128]{2,1,0:T(2,128)(2,1)S(1)} %bitcast.16), channel_id=1, replica_groups=mesh['bucket'=8,'member'=16] {'member'}, dimensions={0}, use_global_device_ids=true | all-gather | bytes 4352 | tf_op jit(solution)/shard_map/all_gather | solution.py:49
  68.6 86.1 %all-gather.3.cloned.1.call-done = bf16[2048,4096]{1,0:T(8,128)(2,1)} async-done(((bf16[128,4096]{1,0:T(8,128)(2,1)}), bf16[2048,4096]{1,0:T(8,128)(2,1)}) %all-gather.3.cloned.1.call-update) | async-done | bytes 16777232 | tf_op jit(solution)/shard_map/all_gather | solution.py:48
  154.8 7.5 %multiply_reduce_fusion = f32[2048]{0:T(1024)S(1)} fusion(bf16[2048,4096]{1,0:T(8,128)(2,1)} %all-gather.3.cloned.1.call-done), kind=kLoop, calls=%fused_computation.4 | loop fusion | flops 25163776 | bytes 16785408 | tf_op jit(solution)/shard_map/reduce_sum | solution.py:18
  162.3 3.1 copy-done
  165.4 7.8 %fusion.2 = (f32[2048]{0:T(1024)S(1)}, f32[2048,256]{1,0:T(8,128)S(1)}) fusion(bf16[2048,4096]{1,0:T(8,128)(2,1)S(1)} %copy-done, f32[256,4096]{1,0:T(8,128)} %param.7, f32[256]{0:T(256)S(1)} %multiply_reduce_fusion.1, f32[2048]{0:T(1024)S(1)} %multiply_reduce_fusion), kind=kOutput, calls=%fused_computation.30 | convolution fusion | flops 4299683840 | bytes 23086080 | tf_op jit(solution)/shard_map/dot_general | solution.py:13
  173.2 39.1 %pmax.28 = f32[2048]{0:T(1024)S(1)} all-reduce(f32[2048]{0:T(1024)S(1)} %get-tuple-element.5), channel_id=1, replica_groups=mesh['bucket'=8,'member'=16] {'member'}, use_global_device_ids=true, to_apply=%region_9.10 | all-reduce | flops 2048 | bytes 16384 | tf_op jit(solution)/shard_map/pmax | solution.py:59
  212.4 0.8 exponential_reduce_fusion.3
  213.1 36.0 %psum.28 = f32[2048]{0:T(1024)S(1)} all-reduce(f32[2048]{0:T(1024)S(1)} %exponential_reduce_fusion.3), channel_id=1, replica_groups=mesh['bucket'=8,'member'=16] {'member'}, use_global_device_ids=true, to_apply=%region_11.12 | all-reduce | flops 2048 | bytes 16384 | tf_op jit(solution)/shard_map/psum | solution.py:60
  249.9 0.7 select_reduce_fusion.5
  250.9 38.0 %pmax.29 = f32[2048]{0:T(1024)S(1)} all-reduce(f32[2048]{0:T(1024)S(1)} %fusion.3), channel_id=1, replica_groups=mesh['bucket'=8,'member'=16] {'member'}, use_global_device_ids=true, to_apply=%region_15.16 | all-reduce | flops 2048 | bytes 16384 | tf_op jit(solution)/shard_map/pmax | solution.py:59
  288.9 0.8 exponential_reduce_fusion.2
  289.8 36.0 %psum.29 = f32[2048]{0:T(1024)S(1)} all-reduce(f32[2048]{0:T(1024)S(1)} %exponential_reduce_fusion.2), channel_id=1, replica_groups=mesh['bucket'=8,'member'=16] {'member'}, use_global_device_ids=true, to_apply=%region_17.18 | all-reduce | flops 2048 | bytes 16384 | tf_op jit(solution)/shard_map/psum | solution.py:60
  327.6 38.0 %pmax.30 = f32[2048]{0:T(1024)S(1)} all-reduce(f32[2048]{0:T(1024)S(1)} %fusion.4), channel_id=1, replica_groups=mesh['bucket'=8,'member'=16] {'member'}, use_global_device_ids=true, to_apply=%region_21.22 | all-reduce | flops 2048 | bytes 16384 | tf_op jit(solution)/shard_map/pmax | solution.py:59
  365.5 0.8 exponential_reduce_fusion.1
  366.4 36.1 %psum.30 = f32[2048]{0:T(1024)S(1)} all-reduce(f32[2048]{0:T(1024)S(1)} %exponential_reduce_fusion.1), channel_id=1, replica_groups=mesh['bucket'=8,'member'=16] {'member'}, use_global_device_ids=true, to_apply=%region_23.24 | all-reduce | flops 2048 | bytes 16384 | tf_op jit(solution)/shard_map/psum | solution.py:60
  403.2 0.7 select_reduce_fusion.1
  404.3 38.0 %pmax.31 = f32[2048]{0:T(1024)S(1)} all-reduce(f32[2048]{0:T(1024)S(1)} %fusion.5), channel_id=1, replica_groups=mesh['bucket'=8,'member'=16] {'member'}, use_global_device_ids=true, to_apply=%region_27.28 | all-reduce | flops 2048 | bytes 16384 | tf_op jit(solution)/shard_map/pmax | solution.py:59
  442.3 0.8 exponential_reduce_fusion
  443.1 36.2 %psum.31 = f32[2048]{0:T(1024)S(1)} all-reduce(f32[2048]{0:T(1024)S(1)} %exponential_reduce_fusion), channel_id=1, replica_groups=mesh['bucket'=8,'member'=16] {'member'}, use_global_device_ids=true, to_apply=%region_29.30 | all-reduce | flops 2048 | bytes 16384 | tf_op jit(solution)/shard_map/psum | solution.py:60
  480.0 0.7 fusion.6
  480.8 12.6 %fusion.7 = f32[256,4096]{1,0:T(8,128)} fusion(bf16[2048,4096]{1,0:T(8,128)(2,1)} %all-gather.3.cloned.1.call-done, f32[2048,256]{1,0:T(8,128)S(1)} %get-tuple-element.6, f32[256]{0:T(256)S(1)} %fusion.6, f32[256]{0:T(256)S(1)} %select_reduce_fusion, f32[2048]{0:T(1024)S(1)} %add_multiply_fusion, pred[2048]{0:T(1024)(128)(4,1)S(1)} %compare_bitcast_fusion), kind=kOutput, calls=%fused_computation.35 | convolution fusion | flops 4298113024 | bytes 23080960 | tf_op jit(solution)/shard_map/dot_general | solution.py:68
  (27 shorter events, 7.6 us)
Async XLA Ops:
  10.5 9.8 %all-to-all-start = ((s32[8,16,1]{1,2,0:T(1,128)}), s32[8,16,1]{1,2,0:T(1,128)S(1)}, u32[]{:S(2)}, u32[]{:S(2)}) async-start(s32[8,16,1]{1,2,0:T(1,128)} %bitcast), calls=%async_computation | async-start | bytes 8192 | tf_op jit(solution)/shard_map/all_to_all | solution.py:36
  20.3 19.5 %all-to-all-start.1 = ((bf16[8,16,4096]{2,1,0:T(8,128)(2,1)}), bf16[8,16,4096]{2,1,0:T(8,128)(2,1)S(1)}, u32[]{:S(2)}, u32[]{:S(2)}) async-start(bf16[8,16,4096]{2,1,0:T(8,128)(2,1)} %bitcast.4), calls=%async_computation.1 | async-start | bytes 2097152 | tf_op jit(solution)/shard_map/all_to_all | solution.py:35
  23.8 130.9 %all-gather.3.cloned.1.call-start = ((), (), s32[]{:S(2)}) async-start(), calls=%async_computation.2 | async-start | bytes 17825792 | tf_op jit(solution)/shard_map/all_gather | solution.py:48
  154.8 10.7 %copy-start = (bf16[2048,4096]{1,0:T(8,128)(2,1)S(1)}, bf16[2048,4096]{1,0:T(8,128)(2,1)}, u32[]{:S(2)}) copy-start(bf16[2048,4096]{1,0:T(8,128)(2,1)} %all-gather.3.cloned.1.call-done) | copy-start | bytes 50331652
Sparse Core Ops, SparseCore 0:
  42.9 111.8 all-gather.2
where the time goes:
time: 501 us; the launch traced here: 500 us
  blocking collectives  319 us (64%)
  waiting for transfers between devices  103 us (21%)
  other arithmetic  26.2 us (5%)
  matrix products  20.4 us (4%)
  between operations  13.7 us (3%)
  local copies, waits for them, and re-layouts  9.75 us (2%)
  starting transfers between devices  8.15 us (2%)
    pmax x4, blocking collectives, body(): row_peak = lax.pmax(local_peak, 'member')  153 us
    psum x4, blocking collectives, body(): lax.psum(jnp.sum(jnp.exp(scores - row_peak[:, None]), axis=1), 'member')  144 us
    all_gather x1, waiting for transfers between devices, body(): lax.all_gather(data_rows, 'member', axis=0, tiled=True)  86.1 us
    all_gather x1, blocking collectives, body(): lax.all_gather(live_rows, 'member', axis=0, tiled=True)  21.9 us
    all_to_all x1, waiting for transfers between devices, body(): lax.all_to_all(send_rows, 'bucket', split_axis=0, concat_axis=0, tiled=True)  14.4 us
    dot_general x1, matrix products, body(): lax.dot_general(weights, whole_rows, (((0,), (0,)), ((), ())), preferred_...  12.6 us
  transfers between devices with their start and end apart: 3, of which 3 were waited for; matrix products, arithmetic and copies ran while one was open for 2% of the time, Pallas kernels for 0%

commit v1 on v0

v1 whole, which is shorter than its diff:
```python
import functools
import math

import jax
import jax.numpy as jnp
from jax import lax
from jax.experimental import pallas as pl
from jax.experimental.pallas import tpu as pltpu
from jax.sharding import PartitionSpec as P

ROWS_DEV = 128
ITERS = 4
SIDE = 4
LANES = 128
EMPTY = 16384.0
MESH = pl.DeviceIdType.MESH
CONTRACT_LAST = (((1,), (1,)), ((), ()))


def pairing_kernel(
    width,
    xs_ref,
    live_ref,
    noise_ref,
    out_ref,
    rows,
    cost,
    noise_wide,
    noise_rows,
    row_norm,
    col_shift,
    row_shift,
    weights,
    lse_out,
    lse_in,
    noise_sem,
    own_sem,
    first_send,
    first_recv,
    second_send,
    second_recv,
    lse_send,
    lse_recv,
):
    members = SIDE * SIDE
    capacity = xs_ref.shape[1]
    noise_count = noise_wide.shape[0]
    part_width = width // members
    tiles = capacity // LANES
    scale = 1.0 / (width * (0.64 / math.sqrt(width)))
    me = lax.axis_index("member")
    my_z, my_x = me // SIDE, me % SIDE

    def member_at(part, first, second):
        along_x, along_z = (first, second) if part == 0 else (second, first)
        return ((my_z + along_z + SIDE) % SIDE) * SIDE + (my_x + along_x + SIDE) % SIDE

    chunk = width // 4
    noise_copies = []
    for k in range(4):
        copy = pltpu.make_async_copy(
            noise_ref.at[:, pl.ds(k * chunk, chunk)],
            noise_wide.at[:, pl.ds(k * chunk, chunk)],
            noise_sem.at[k],
        )
        copy.start()
        noise_copies.append(copy)
    own_copy = pltpu.make_async_copy(xs_ref, rows.at[me], own_sem)
    own_copy.start()

    barrier = pltpu.get_barrier_semaphore()
    for k in range(1, members):
        pl.semaphore_signal(
            barrier, inc=1, device_id={"member": (me + k) % members}, device_id_type=MESH
        )
    pl.semaphore_wait(barrier, members - 1)

    half, quarter = capacity // 2, capacity // 4
    units = [(0, 0, capacity), (-1, 0, capacity), (1, 0, capacity), (2, 0, half), (2, half, half)]
    ways = (1, -1)
    pending = {}

    def send(label, part, owner, start, count, neighbour, sems, own=False):
        source = xs_ref.at[part] if own else rows.at[owner, part]
        copy = pltpu.make_async_remote_copy(
            src_ref=source.at[pl.ds(start, count)],
            dst_ref=rows.at[owner, part, pl.ds(start, count)],
            send_sem=sems[0],
            recv_sem=sems[1],
            device_id={"member": neighbour},
            device_id_type=MESH,
        )
        copy.start()
        pending[label] = copy

    def first_hop(part, d):
        sems = (first_send.at[part, 0, d], first_recv.at[part, 0, d])
        send(("f1", part, d), part, me, 0, capacity, member_at(part, ways[d], 0), sems, True)

    def first_forward(part, d):
        sems = (first_send.at[part, 1, d], first_recv.at[part, 1, d])
        owner = member_at(part, -ways[d], 0)
        send(("f2", part, d), part, owner, d * half, half, member_at(part, ways[d], 0), sems)

    def second_hop(part, u, d):
        first, start, count = units[u]
        sems = (second_send.at[part, 0, u, d], second_recv.at[part, 0, u, d])
        owner = me if u == 0 else member_at(part, first, 0)
        send(("g1", part, u, d), part, owner, start, count, member_at(part, 0, ways[d]), sems, u == 0)

    def second_forward(part, u, d):
        first, start, count = units[u]
        sems = (second_send.at[part, 1, u, d], second_recv.at[part, 1, u, d])
        owner = member_at(part, first, -ways[d])
        send(
            ("g2", part, u, d), part, owner, start + d * (count // 2), count // 2,
            member_at(part, 0, ways[d]), sems,
        )

    def arrive(label):
        pending[label].wait_recv()

    def add_slice(owner):
        panel = jnp.concatenate([rows[owner, 0], rows[owner, 1]], axis=1)
        cost[...] += lax.dot_general(
            noise_rows[owner], panel, CONTRACT_LAST, preferred_element_type=jnp.float32
        )
        wide = panel.astype(jnp.float32)
        square = wide * wide
        high = square.astype(jnp.bfloat16)
        low = (square - high.astype(jnp.float32)).astype(jnp.bfloat16)
        ones = jnp.ones((8, panel.shape[1]), jnp.bfloat16)
        row_norm[...] += lax.dot_general(
            ones, high, CONTRACT_LAST, preferred_element_type=jnp.float32
        ) + lax.dot_general(ones, low, CONTRACT_LAST, preferred_element_type=jnp.float32)

    for part in range(2):
        for d in range(2):
            first_hop(part, d)
    for part in range(2):
        for d in range(2):
            second_hop(part, 0, d)

    cost[...] = jnp.zeros_like(cost)
    row_norm[...] = jnp.zeros_like(row_norm)
    per_chunk = chunk // part_width
    noise_norm = jnp.zeros((noise_count, 1), jnp.float32)
    for k in range(4):
        noise_copies[k].wait()
        for s in range(per_chunk):
            q = k * per_chunk + s
            block = noise_wide[:, q * part_width : (q + 1) * part_width].astype(jnp.bfloat16)
            noise_rows[q] = block
            wide = block.astype(jnp.float32)
            noise_norm += jnp.sum(wide * wide, axis=1, keepdims=True)
    own_copy.wait()
    add_slice(me)

    for part in range(2):
        for d in range(2):
            arrive(("f1", part, d))
            first_forward(part, d)
            u = 1 if d == 0 else 2
            for e in range(2):
                second_hop(part, u, e)
    for part in range(2):
        for d in range(2):
            arrive(("g1", part, 0, d))
            second_forward(part, 0, d)
    for step in ways:
        add_slice(member_at(0, step, 0))
        add_slice(member_at(0, 0, step))
    for d in range(2):
        for part in range(2):
            arrive(("f2", part, d))
            for e in range(2):
                second_hop(part, 3 + d, e)
    for u in (1, 2):
        for part in range(2):
            for d in range(2):
                arrive(("g1", part, u, d))
                second_forward(part, u, d)
    for step in ways:
        for other in ways:
            add_slice(member_at(0, step, other))
    for u in (3, 4):
        for part in range(2):
            for d in range(2):
                arrive(("g1", part, u, d))
                second_forward(part, u, d)
    for part in range(2):
        for d in range(2):
            arrive(("g2", part, 0, d))
    for part in range(2):
        add_slice(member_at(part, 2, 0))
    for u in (1, 2):
        for part in range(2):
            for d in range(2):
                arrive(("g2", part, u, d))
        for part in range(2):
            add_slice(member_at(part, units[u][0], 2))
    for u in (3, 4):
        for part in range(2):
            for d in range(2):
                arrive(("g2", part, u, d))
    add_slice(member_at(0, 2, 2))
    for copy in pending.values():
        copy.wait_send()

    for t in range(tiles):
        lanes = slice(t * LANES, (t + 1) * LANES)
        cost[:, lanes] = (2.0 * cost[:, lanes] - row_norm[0:1, lanes] - noise_norm) * scale

    col_shift[...] = jnp.zeros_like(col_shift)
    row_chunk = 32
    for it in range(ITERS):
        for t in range(tiles):
            lanes = slice(t * LANES, (t + 1) * LANES)
            scores = cost[:, lanes] + col_shift[...]
            peak = jnp.max(scores, axis=0, keepdims=True)
            total = jnp.sum(jnp.exp(scores - peak), axis=0, keepdims=True)
            lse_out[it, t : t + 1, :] = peak + jnp.log(total)
        lse_copies = []
        for k in range(1, members):
            copy = pltpu.make_async_remote_copy(
                src_ref=lse_out.at[it],
                dst_ref=lse_in.at[it, k],
                send_sem=lse_send.at[it, k],
                recv_sem=lse_recv.at[it, k],
                device_id={"member": (me + k) % members},
                device_id_type=MESH,
            )
            copy.start()
            lse_copies.append(copy)
        for copy in lse_copies:
            copy.wait_recv()
        peak = lse_out[it]
        for k in range(1, members):
            peak = jnp.maximum(peak, lse_in[it, k])
        total = jnp.exp(lse_out[it] - peak)
        for k in range(1, members):
            total += jnp.exp(lse_in[it, k] - peak)
        shift = -(peak + jnp.log(total))
        for t in range(tiles):
            lanes = slice(t * LANES, (t + 1) * LANES)
            row_shift[0:1, lanes] = jnp.where(live_ref[0:1, lanes] > 0.5, shift[t : t + 1, :], -jnp.inf)
        for c in range(noise_count // row_chunk):
            span = slice(c * row_chunk, (c + 1) * row_chunk)
            scores = cost[span, :] + row_shift[0:1, :]
            peak = jnp.max(scores, axis=1, keepdims=True)
            exponent = jnp.exp(scores - peak)
            total = jnp.sum(exponent, axis=1, keepdims=True)
            if it < ITERS - 1:
                col_shift[span, :] = jnp.broadcast_to(-(peak + jnp.log(total)), (row_chunk, LANES))
            else:
                weights[span, :] = (exponent / total).astype(jnp.bfloat16)
        for copy in lse_copies:
            copy.wait_send()

    @pl.loop(0, members)
    def _(q):
        panel = jnp.concatenate([rows[q, 0], rows[q, 1]], axis=1)
        start = pl.multiple_of(q * part_width, part_width)
        out_ref[:, pl.ds(start, part_width)] = jnp.dot(
            weights[...], panel, preferred_element_type=jnp.float32
        )


def pair(xs, live, noise):
    members = SIDE * SIDE
    capacity = xs.shape[1]
    noise_count, width = noise.shape
    tiles = capacity // LANES
    part_width = width // members
    dma = pltpu.SemaphoreType.DMA
    return pl.pallas_call(
        functools.partial(pairing_kernel, width),
        out_shape=jax.ShapeDtypeStruct((noise_count, width), jnp.float32),
        in_specs=[
            pl.BlockSpec(memory_space=pltpu.VMEM),
            pl.BlockSpec(memory_space=pltpu.VMEM),
            pl.BlockSpec(memory_space=pl.ANY),
        ],
        out_specs=pl.BlockSpec(memory_space=pltpu.VMEM),
        scratch_shapes=[
            pltpu.VMEM((members, 2, capacity, LANES), jnp.bfloat16),
            pltpu.VMEM((noise_count, capacity), jnp.float32),
            pltpu.VMEM((noise_count, width), jnp.float32),
            pltpu.VMEM((members, noise_count, part_width), jnp.bfloat16),
            pltpu.VMEM((8, capacity), jnp.float32),
            pltpu.VMEM((noise_count, LANES), jnp.float32),
            pltpu.VMEM((8, capacity), jnp.float32),
            pltpu.VMEM((noise_count, capacity), jnp.bfloat16),
            pltpu.VMEM((ITERS, tiles, LANES), jnp.float32),
            pltpu.VMEM((ITERS, members, tiles, LANES), jnp.float32),
            dma((4,)),
            dma,
            dma((2, 2, 2)),
            dma((2, 2, 2)),
            dma((2, 2, 5, 2)),
            dma((2, 2, 5, 2)),
            dma((ITERS, members)),
            dma((ITERS, members)),
        ],
        compiler_params=pltpu.CompilerParams(
            collective_id=0, has_side_effects=True, vmem_limit_bytes=60 * 1024 * 1024
        ),
    )(xs, live, noise)


def body(loader_rows, dest_bucket, dest_slot, noise):
    groups = lax.axis_size("bucket")
    members = lax.axis_size("member")
    loaded, width = loader_rows.shape
    capacity = ROWS_DEV // groups
    rounded = loader_rows.astype(jnp.bfloat16)
    index = jnp.arange(loaded, dtype=jnp.int32)
    earlier = (dest_bucket[:, None] == dest_bucket[None, :]) & (index[None, :] < index[:, None])
    position = dest_bucket * capacity + jnp.sum(earlier.astype(jnp.int32), axis=1)
    hits = position[None, :] == jnp.arange(groups * capacity, dtype=jnp.int32)[:, None]
    packed = jnp.dot(hits.astype(jnp.bfloat16), rounded, preferred_element_type=jnp.float32)
    filled = jnp.any(hits, axis=1)
    packed = jnp.where(filled[:, None], packed, EMPTY).astype(jnp.bfloat16)
    packed = packed.reshape(groups, capacity, members, width // members)
    packed = packed.transpose(0, 2, 1, 3).reshape(groups * members, capacity, width // members)
    got = lax.all_to_all(packed, ("bucket", "member"), split_axis=0, concat_axis=0, tiled=True)
    got = got.reshape(groups * members * capacity, width // members)
    live = got[:, 0] < 0.5 * EMPTY
    got = jnp.where(live[:, None], got, jnp.zeros_like(got))
    xs = jnp.stack([got[:, :LANES], got[:, LANES:]])
    live_rows = jnp.broadcast_to(live.astype(jnp.float32)[None, :], (8, live.shape[0]))
    return pair(xs, live_rows, noise)


def solution(mesh):
    return jax.shard_map(
        body,
        mesh=mesh,
        in_specs=(
            P(("bucket", "member"), None),
            P(("bucket", "member")),
            P(("bucket", "member")),
            P(("bucket", "member"), None),
        ),
        out_specs=P(("bucket", "member"), None),
        check_vma=False,
    )
```

time: 501 us -> 169 us (0.34)
  blocking collectives: 319 us -> 30 us
  Pallas kernels: 0 us -> 128 us
  waiting for transfers between devices: 103 us -> 0 us
  other arithmetic: 26.2 us -> 3.63 us
  matrix products: 20.4 us -> 1.77 us
  between operations: 13.7 us -> 0.07 us
  starting transfers between devices: 8.15 us -> 0 us
    pmax x4 -> x0, blocking collectives: 153 us -> none  [body(): row_peak = lax.pmax(local_peak, 'member')]
    psum x4 -> x0, blocking collectives: 144 us -> none  [body(): lax.psum(jnp.sum(jnp.exp(scores - row_peak[:, None]), axis=1), 'member')]
    pallas_call x0 -> x1, Pallas kernels: none -> 128 us  [pair(): pl.pallas_call(functools.partial(pairing_kernel, width), out_shape=jax.Sh...]
    all_gather x1 -> x0, waiting for transfers between devices: 86.1 us -> none  [body(): lax.all_gather(data_rows, 'member', axis=0, tiled=True)]
    all_to_all x0 -> x1, blocking collectives: none -> 30 us  [body(): lax.all_to_all(packed, ('bucket', 'member'), split_axis=0, concat_axis=0,...]
    all_gather x1 -> x0, blocking collectives: 21.9 us -> none  [body(): lax.all_gather(live_rows, 'member', axis=0, tiled=True)]
    dot_general x2 -> x1, matrix products: 20.4 us -> 1.77 us  [body(): jnp.dot(hits.astype(jnp.bfloat16), rounded, preferred_element_type=jnp.fl...]
    all_to_all x2 -> x0, waiting for transfers between devices: 16.6 us -> none  [the longest x1 14.4 us: body(): lax.all_to_all(send_rows, 'bucket', split_axis=0, concat_axis=0, tiled=True)]
  transfers between devices with their start and end apart: 3 -> 0, of which waited for: 3 -> 0; matrix products, arithmetic and copies ran while one was open for 2% -> 0% of each run, Pallas kernels for 0% -> 0%
where the time goes in v1:
time: 169 us
  Pallas kernels  128 us (76%)
  blocking collectives  30 us (18%)
  local copies, waits for them, and re-layouts  6.07 us (4%)
  other arithmetic  3.63 us (2%)
  matrix products  1.77 us (1%)
    pallas_call x1, Pallas kernels, pair(): pl.pallas_call(functools.partial(pairing_kernel, width), out_shape=jax.Sh...  128 us
    all_to_all x1, blocking collectives, body(): lax.all_to_all(packed, ('bucket', 'member'), split_axis=0, concat_axis=0,...  30 us
    unnamed x2, local copies, waits for them, and re-layouts  4.9 us

profile of v1, /device:TPU:0, one launch (start us, length us, event | category | flops | bytes accessed | tf_op | source)
XLA Modules:
  0.0 169.2 jit_solution(11083819158862276218)
XLA Ops:
  0.0 0.9 convert_reduce_fusion
  0.9 0.7 multiply_add_fusion
  1.6 0.1 fusion.2
  1.7 1.8 %fusion = bf16[128,4096]{1,0:T(8,128)(2,1)S(1)} fusion(pred[128]{0:T(512)(128)(4,1)S(1)} %fusion.2, f32[64,4096]{1,0:T(8,128)} %param.4, s32[64]{0:T(128)S(1)} %multiply_add_fusion), kind=kOutput, calls=%fused_computation.1 | convolution fusion | flops 68427776 | bytes 2097536 | tf_op jit(solution)/shard_map/dot_general | solution.py:321
  3.5 0.2 copy.7
  3.7 0.1 bitcast_bitcast_fusion
  3.8 0.4 copy.6
  4.2 30.0 %all_to_all.5 = bf16[128,16,256]{2,1,0:T(8,128)(2,1)S(1)} all-to-all(bf16[128,16,256]{2,1,0:T(8,128)(2,1)S(1)} %bitcast.16), channel_id=1, replica_groups=mesh['bucket'=8,'member'=16] {'bucket','member'}, dimensions={0} | all-to-all | bytes 2097152 | tf_op jit(solution)/shard_map/all_to_all | solution.py:326
  34.2 0.4 compare_reduce_fusion
  34.5 0.5 broadcast_select_fusion
  35.1 0.1 slice_bitcast_fusion.1
  35.2 1.1 pad_maximum_fusion.xs_ref
  36.2 0.6 broadcast_in_dim.44.live_ref
  36.9 127.7 %shard_map.37 = f32[256,4096]{1,0:T(8,128)} custom-call(bf16[2,2048,128]{2,1,0:T(8,128)(2,1)} %pad_maximum_fusion.xs_ref, f32[8,2048]{1,0:T(8,128)} %broadcast_in_dim.44.live_ref, f32[256,4096]{1,0:T(8,128)} %noise_ref.1), custom_call_target="tpu_custom_call" | custom-call | tf_op jit(solution)/shard_map/pallas_call | solution.py:276
  164.5 4.7 %copy.9 = f32[256,4096]{1,0:T(8,128)} copy(f32[256,4096]{1,0:T(8,128)} %shard_map.37) | data formatting | bytes 8388608
  (1 shorter events, 0.0 us)

commit v2 on v1

--- a/solution.py
+++ b/solution.py
@@ -11,6 +11,8 @@
 ROWS_DEV = 128
 ITERS = 4
 SIDE = 4
+BUCKETS = 8
+FAST_ROWS = 1152
 LANES = 128
 EMPTY = 16384.0
 MESH = pl.DeviceIdType.MESH
@@ -266,7 +268,7 @@
         )
 
 
-def pair(xs, live, noise):
+def pair(xs, live, noise, collective_id):
     members = SIDE * SIDE
     capacity = xs.shape[1]
     noise_count, width = noise.shape
@@ -303,33 +305,243 @@
             dma((ITERS, members)),
         ],
         compiler_params=pltpu.CompilerParams(
-            collective_id=0, has_side_effects=True, vmem_limit_bytes=60 * 1024 * 1024
+            collective_id=collective_id, has_side_effects=True, vmem_limit_bytes=60 * 1024 * 1024
         ),
     )(xs, live, noise)
 
 
+def routing_kernel(
+    dest_ref,
+    loaded_ref,
+    slots_ref,
+    live_ref,
+    count_ref,
+    packed,
+    landed,
+    position,
+    tally,
+    tally_bucket,
+    tally_member,
+    bucket_send,
+    bucket_recv,
+    member_send,
+    member_recv,
+    tally_send,
+    tally_recv,
+):
+    groups, members = BUCKETS, SIDE * SIDE
+    loaded, width = loaded_ref.shape
+    part_width = width // members
+    block = ROWS_DEV // groups
+    fast_rows = live_ref.shape[1]
+    my_bucket, me = lax.axis_index("bucket"), lax.axis_index("member")
+
+    barrier = pltpu.get_barrier_semaphore()
+    for k in range(1, groups):
+        pl.semaphore_signal(
+            barrier, inc=1, device_id={"bucket": (my_bucket + k) % groups}, device_id_type=MESH
+        )
+    for k in range(1, members):
+        pl.semaphore_signal(
+            barrier, inc=1, device_id={"member": (me + k) % members}, device_id_type=MESH
+        )
+
+    dest = dest_ref[...]
+    of_bucket = lax.broadcasted_iota(jnp.int32, (groups, loaded), 0) == dest
+    hits = of_bucket.astype(jnp.float32)
+    up_to = (
+        lax.broadcasted_iota(jnp.int32, (loaded, loaded), 0)
+        <= lax.broadcasted_iota(jnp.int32, (loaded, loaded), 1)
+    ).astype(jnp.bfloat16)
+    ranks = jnp.dot(hits.astype(jnp.bfloat16), up_to, preferred_element_type=jnp.float32)
+    place = jnp.sum(hits * (ranks - 1.0), axis=0, keepdims=True).astype(jnp.int32) + dest * block
+    pick = lax.broadcasted_iota(jnp.int32, (ROWS_DEV, loaded), 0) == place
+    pick = pick.astype(jnp.float32)
+    fill = EMPTY * (1.0 - jnp.sum(pick, axis=1, keepdims=True))
+    pick = pick.astype(jnp.bfloat16)
+    tally[0] = jnp.broadcast_to(jnp.sum(hits, axis=1, keepdims=True), tally.shape[1:])
+
+    def pack(c):
+        for k in range(4 * c, 4 * c + 4):
+            start = pl.multiple_of(((me + k) % members) * part_width, part_width)
+            panel = loaded_ref[:, pl.ds(start, part_width)].astype(jnp.bfloat16)
+            sorted_panel = jnp.dot(pick, panel, preferred_element_type=jnp.float32) + fill
+            sorted_panel = sorted_panel.astype(jnp.bfloat16)
+            for part in range(2):
+                packed[k, part] = sorted_panel[:, part * LANES : (part + 1) * LANES]
+
+    def block_of(bucket):
+        return pl.ds(pl.multiple_of(bucket * block, block), block)
+
+    bucket_copies = {}
+
+    def send_quarter(c):
+        quarter = pl.ds(4 * c, 4)
+        for k in range(1, groups):
+            peer = (my_bucket + k) % groups
+            copy = pltpu.make_async_remote_copy(
+                src_ref=packed.at[quarter, :, block_of(peer)],
+                dst_ref=landed.at[quarter, :, block_of(my_bucket)],
+                send_sem=bucket_send.at[c, k],
+                recv_sem=bucket_recv.at[c, k],
+                device_id={"bucket": peer},
+                device_id_type=MESH,
+            )
+            copy.start()
+            bucket_copies[c, k] = copy
+        landed[quarter, :, block_of(my_bucket), :] = packed[quarter, :, block_of(my_bucket), :]
+
+    pack(0)
+    pl.semaphore_wait(barrier, groups + members - 2)
+    send_quarter(0)
+    tally_copies = []
+    for k in range(1, groups):
+        copy = pltpu.make_async_remote_copy(
+            src_ref=tally.at[0],
+            dst_ref=tally_bucket.at[k],
+            send_sem=tally_send.at[0, k],
+            recv_sem=tally_recv.at[0, k],
+            device_id={"bucket": (my_bucket + k) % groups},
+            device_id_type=MESH,
+        )
+        copy.start()
+        tally_copies.append(copy)
+    for c in range(1, 4):
+        pack(c)
+        send_quarter(c)
+    my_rows = pl.ds(pl.multiple_of(me * ROWS_DEV, ROWS_DEV), ROWS_DEV)
+    member_copies = []
+    for c in range(4):
+        for k in range(1, groups):
+            bucket_copies[c, k].wait_recv()
+        for k in range(4 * c, 4 * c + 4):
+            if k == 0:
+                slots_ref[:, my_rows, :] = landed[0]
+                continue
+            copy = pltpu.make_async_remote_copy(
+                src_ref=landed.at[k],
+                dst_ref=slots_ref.at[:, my_rows],
+                send_sem=member_send.at[k],
+                recv_sem=member_recv.at[k],
+                device_id={"member": (me + k) % members},
+                device_id_type=MESH,
+            )
+            copy.start()
+            member_copies.append(copy)
+        if c == 0:
+            total = tally[0]
+            for k in range(1, groups):
+                tally_copies[k - 1].wait_recv()
+                total += tally_bucket[k]
+            tally[1] = total
+            for k in range(1, members):
+                copy = pltpu.make_async_remote_copy(
+                    src_ref=tally.at[1],
+                    dst_ref=tally_member.at[k],
+                    send_sem=tally_send.at[1, k],
+                    recv_sem=tally_recv.at[1, k],
+                    device_id={"member": (me + k) % members},
+                    device_id_type=MESH,
+                )
+                copy.start()
+                tally_copies.append(copy)
+    total = tally[1]
+    for k in range(1, members):
+        tally_copies[groups - 2 + k].wait_recv()
+        total += tally_member[k]
+    count_ref[...] = total
+    for copy in member_copies:
+        copy.wait_recv()
+
+    marks = lax.dot_general(
+        jnp.ones((8, LANES), jnp.bfloat16), slots_ref[0], CONTRACT_LAST,
+        preferred_element_type=jnp.float32,
+    )
+    for t in range(members):
+        lanes = slice(t * LANES, (t + 1) * LANES)
+        position[t : t + 1, :] = (marks[0:1, lanes] < 0.5 * LANES * EMPTY).astype(jnp.float32)
+    alive = position[...]
+    before = (
+        lax.broadcasted_iota(jnp.int32, (LANES, LANES), 0)
+        <= lax.broadcasted_iota(jnp.int32, (LANES, LANES), 1)
+    ).astype(jnp.bfloat16)
+    inside = jnp.dot(alive.astype(jnp.bfloat16), before, preferred_element_type=jnp.float32)
+    per_member = jnp.broadcast_to(inside[:, LANES - 1 : LANES], (members, LANES))
+    earlier = (
+        lax.broadcasted_iota(jnp.int32, (members, members), 0)
+        > lax.broadcasted_iota(jnp.int32, (members, members), 1)
+    ).astype(jnp.bfloat16)
+    offset = jnp.dot(earlier, per_member.astype(jnp.bfloat16), preferred_element_type=jnp.float32)
+    position[...] = jnp.where(alive > 0.5, inside + offset - 1.0, -1.0)
+    step = fast_rows // 3
+
+    @pl.loop(0, 3)
+    def _(c):
+        start = pl.multiple_of(c * step, step)
+        target = (lax.broadcasted_iota(jnp.int32, (step, LANES), 0) + start).astype(jnp.float32)
+        choose = jnp.concatenate(
+            [(target == position[t : t + 1, :]).astype(jnp.bfloat16) for t in range(members)], axis=1
+        )
+        for part in range(2):
+            live_ref[part, pl.ds(start, step), :] = jnp.dot(
+                choose, slots_ref[part], preferred_element_type=jnp.float32
+            ).astype(jnp.bfloat16)
+
+    for copy in list(bucket_copies.values()) + tally_copies + member_copies:
+        copy.wait_send()
+
+
+def route(dest_bucket, loader_rows):
+    members = SIDE * SIDE
+    width = loader_rows.shape[1]
+    dma = pltpu.SemaphoreType.DMA
+    vmem = pl.BlockSpec(memory_space=pltpu.VMEM)
+    slot_rows = members * ROWS_DEV
+    return pl.pallas_call(
+        routing_kernel,
+        out_shape=(
+            jax.ShapeDtypeStruct((2, slot_rows, LANES), jnp.bfloat16),
+            jax.ShapeDtypeStruct((2, FAST_ROWS, LANES), jnp.bfloat16),
+            jax.ShapeDtypeStruct((BUCKETS, LANES), jnp.float32),
+        ),
+        in_specs=[vmem, vmem],
+        out_specs=(vmem, vmem, vmem),
+        scratch_shapes=[
+            pltpu.VMEM((members, 2, ROWS_DEV, LANES), jnp.bfloat16),
+            pltpu.VMEM((members, 2, ROWS_DEV, LANES), jnp.bfloat16),
+            pltpu.VMEM((members, LANES), jnp.float32),
+            pltpu.VMEM((2, BUCKETS, LANES), jnp.float32),
+            pltpu.VMEM((BUCKETS, BUCKETS, LANES), jnp.float32),
+            pltpu.VMEM((members, BUCKETS, LANES), jnp.float32),
+            dma((4, BUCKETS)),
+            dma((4, BUCKETS)),
+            dma((members,)),
+            dma((members,)),
+            dma((2, members)),
+            dma((2, members)),
+        ],
+        compiler_params=pltpu.CompilerParams(
+            collective_id=1, has_side_effects=True, vmem_limit_bytes=40 * 1024 * 1024
+        ),
+    )(dest_bucket.reshape(1, -1), loader_rows)
+
+
 def body(loader_rows, dest_bucket, dest_slot, noise):
-    groups = lax.axis_size("bucket")
-    members = lax.axis_size("member")
-    loaded, width = loader_rows.shape
-    capacity = ROWS_DEV // groups
-    rounded = loader_rows.astype(jnp.bfloat16)
-    index = jnp.arange(loaded, dtype=jnp.int32)
-    earlier = (dest_bucket[:, None] == dest_bucket[None, :]) & (index[None, :] < index[:, None])
-    position = dest_bucket * capacity + jnp.sum(earlier.astype(jnp.int32), axis=1)
-    hits = position[None, :] == jnp.arange(groups * capacity, dtype=jnp.int32)[:, None]
-    packed = jnp.dot(hits.astype(jnp.bfloat16), rounded, preferred_element_type=jnp.float32)
-    filled = jnp.any(hits, axis=1)
-    packed = jnp.where(filled[:, None], packed, EMPTY).astype(jnp.bfloat16)
-    packed = packed.reshape(groups, capacity, members, width // members)
-    packed = packed.transpose(0, 2, 1, 3).reshape(groups * members, capacity, width // members)
-    got = lax.all_to_all(packed, ("bucket", "member"), split_axis=0, concat_axis=0, tiled=True)
-    got = got.reshape(groups * members * capacity, width // members)
-    live = got[:, 0] < 0.5 * EMPTY
-    got = jnp.where(live[:, None], got, jnp.zeros_like(got))
-    xs = jnp.stack([got[:, :LANES], got[:, LANES:]])
-    live_rows = jnp.broadcast_to(live.astype(jnp.float32)[None, :], (8, live.shape[0]))
-    return pair(xs, live_rows, noise)
+    slots, compact, counts = route(dest_bucket, loader_rows)
+    group = lax.axis_index("bucket")
+
+    def all_slots(slots, compact, counts, noise):
+        live = (slots[0, :, 0] < 0.5 * EMPTY).astype(jnp.float32)
+        cleared = jnp.where(slots < 0.5 * EMPTY, slots, jnp.zeros_like(slots))
+        return pair(cleared, jnp.broadcast_to(live[None, :], (8, live.shape[0])), noise, 2)
+
+    def live_first(slots, compact, counts, noise):
+        index = lax.broadcasted_iota(jnp.int32, (8, FAST_ROWS), 1).astype(jnp.float32)
+        live = (index < counts[group, 0]).astype(jnp.float32)
+        return pair(compact, live, noise, 0)
+
+    fits = jnp.all(counts <= FAST_ROWS)
+    return lax.cond(fits, live_first, all_slots, slots, compact, counts, noise)
 
 
 def solution(mesh):

time: 169 us -> 134 us (0.79)
  blocking collectives: 30 us -> 0 us
  Pallas kernels: 128 us -> 124 us
  other arithmetic: 3.63 us -> 1.28 us
  matrix products: 1.77 us -> 0 us
    pallas_call x1, Pallas kernels: 128 us -> 87.6 us  [pair(): pl.pallas_call(functools.partial(pairing_kernel, width), out_shape=jax.Sh...]
    pallas_call x0 -> x1, Pallas kernels: none -> 36.3 us  [route(): pl.pallas_call(routing_kernel, out_shape=(jax.ShapeDtypeStruct((2, slot_r...]
    all_to_all x1 -> x0, blocking collectives: 30 us -> none  [body(): lax.all_to_all(packed, ('bucket', 'member'), split_axis=0, concat_axis=0,...]
    dot_general x1 -> x0, matrix products: 1.77 us -> none  [body(): jnp.dot(hits.astype(jnp.bfloat16), rounded, preferred_element_type=jnp.fl...]
    unnamed x2 -> x5, local copies, waits for them, and re-layouts: 4.9 us -> 6.53 us
where the time goes in v2:
time: 134 us
  Pallas kernels  124 us (93%)
  local copies, waits for them, and re-layouts  7.68 us (6%)
    pallas_call x1, Pallas kernels, pair(): pl.pallas_call(functools.partial(pairing_kernel, width), out_shape=jax.Sh...  87.6 us
    pallas_call x1, Pallas kernels, route(): pl.pallas_call(routing_kernel, out_shape=(jax.ShapeDtypeStruct((2, slot_r...  36.3 us
    unnamed x5, local copies, waits for them, and re-layouts  6.53 us

profile of v2, /device:TPU:0, one launch (start us, length us, event | category | flops | bytes accessed | tf_op | source)
XLA Modules:
  0.0 133.7 jit_solution(18214222027200607006)
XLA Ops:
  0.0 0.0 copy-start
  0.0 1.2 copy-done
  1.2 0.0 copy-start.1
  1.2 0.7 copy-done.1
  1.9 36.3 %shard_map.39 = (bf16[2,2048,128]{2,1,0:T(8,128)(2,1)S(1)}, bf16[2,1152,128]{2,1,0:T(8,128)(2,1)S(1)}, f32[8,128]{1,0:T(8,128)S(1)}) custom-call(s32[1,64]{1,0:T(1,128)S(1)} %bitcast.2, f32[64,4096]{1,0:T(8,128)S(1)} %copy-done), custom_call_target="tpu_custom_call" | custom-call | tf_op jit(solution)/shard_map/pallas_call | solution.py:500
  38.2 0.6 compare_reduce_fusion
  39.5 89.6 %conditional.1 = (f32[256,4096]{1,0:T(8,128)}) conditional(s32[]{:T(128)} %convert_element_type.20, (bf16[2,2048,128]{2,1,0:T(8,128)(2,1)S(1)}, f32[256,4096]{1,0:T(8,128)}) %tuple.11, (s32[]{:T(128)}, f32[8,128]{1,0:T(8,128)S(1)}, bf16[2,1152,128]{2,1,0:T(8,128)(2,1)S(1)}, f32[256,4096]{1,0:T(8,128)}) %tuple.12), branch_computations={%region_1.2_spmd, %region_2.3_spmd} | conditional | flops 1052672 | bytes 2183176 | solution.py:544
  39.7 0.5 constant_dynamic-slice_fusion
  40.2 0.6 fusion
  40.9 0.6 iota.5.live_ref
  41.5 87.6 %branch_1_fun.1 = f32[256,4096]{1,0:T(8,128)} custom-call(bf16[2,1152,128]{2,1,0:T(8,128)(2,1)S(1)} %get-tuple-element.22.xs_ref, f32[8,1152]{1,0:T(8,128)} %iota.5.live_ref, f32[256,4096]{1,0:T(8,128)} %get-tuple-element.25.noise_ref), custom_call_target="tpu_custom_call" | custom-call | tf_op jit(solution)/shard_map/cond/branch_1_fun/pallas_call | solution.py:278
  129.1 4.7 %copy.9 = f32[256,4096]{1,0:T(8,128)} copy(f32[256,4096]{1,0:T(8,128)} %get-tuple-element.32) | data formatting | bytes 8388608
Async XLA Ops:
  0.0 1.2 copy-start
  1.2 0.7 copy-start.1

commit v3 on v1

--- a/solution.py
+++ b/solution.py
@@ -11,6 +11,8 @@
 ROWS_DEV = 128
 ITERS = 4
 SIDE = 4
+BUCKETS = 8
+FAST_ROWS = 1120
 LANES = 128
 EMPTY = 16384.0
 MESH = pl.DeviceIdType.MESH
@@ -19,22 +21,23 @@
 
 def pairing_kernel(
     width,
-    xs_ref,
-    live_ref,
+    sent,
+    slots_ref,
+    count_ref,
     noise_ref,
-    out_ref,
     rows,
+    weights,
     cost,
     noise_wide,
     noise_rows,
     row_norm,
+    live,
+    position,
     col_shift,
     row_shift,
-    weights,
     lse_out,
     lse_in,
     noise_sem,
-    own_sem,
     first_send,
     first_recv,
     second_send,
@@ -43,7 +46,7 @@
     lse_recv,
 ):
     members = SIDE * SIDE
-    capacity = xs_ref.shape[1]
+    capacity = rows.shape[2]
     noise_count = noise_wide.shape[0]
     part_width = width // members
     tiles = capacity // LANES
@@ -65,26 +68,91 @@
         )
         copy.start()
         noise_copies.append(copy)
-    own_copy = pltpu.make_async_copy(xs_ref, rows.at[me], own_sem)
-    own_copy.start()
 
     barrier = pltpu.get_barrier_semaphore()
     for k in range(1, members):
         pl.semaphore_signal(
             barrier, inc=1, device_id={"member": (me + k) % members}, device_id_type=MESH
         )
+
+    marks = jnp.concatenate(
+        [
+            lax.dot_general(
+                jnp.ones((8, LANES), jnp.bfloat16), slots_ref[0, t], CONTRACT_LAST,
+                preferred_element_type=jnp.float32,
+            )[0:1]
+            for t in range(members)
+        ],
+        axis=0,
+    )
+    alive = (marks < 0.5 * LANES * EMPTY).astype(jnp.float32)
+    if capacity == members * ROWS_DEV:
+        live[...] = alive
+        for part in range(2):
+            for t in range(members):
+                block = slots_ref[part, t].astype(jnp.float32)
+                block = jnp.where(block < 0.5 * EMPTY, block, 0.0)
+                rows[me, part, t * ROWS_DEV : (t + 1) * ROWS_DEV, :] = block.astype(jnp.bfloat16)
+    else:
+        before = (
+            lax.broadcasted_iota(jnp.int32, (LANES, LANES), 0)
+            <= lax.broadcasted_iota(jnp.int32, (LANES, LANES), 1)
+        ).astype(jnp.bfloat16)
+        inside = jnp.dot(alive.astype(jnp.bfloat16), before, preferred_element_type=jnp.float32)
+        per_member = jnp.broadcast_to(inside[:, LANES - 1 : LANES], (members, LANES))
+        earlier = (
+            lax.broadcasted_iota(jnp.int32, (members, members), 0)
+            > lax.broadcasted_iota(jnp.int32, (members, members), 1)
+        ).astype(jnp.bfloat16)
+        offset = jnp.dot(
+            earlier, per_member.astype(jnp.bfloat16), preferred_element_type=jnp.float32
+        )
+        position[...] = jnp.where(alive > 0.5, inside + offset - 1.0, -1.0)
+        step = capacity // 3
+
+        @pl.loop(0, 3)
+        def _(c):
+            start = pl.multiple_of(c * step, LANES)
+            target = (lax.broadcasted_iota(jnp.int32, (step, LANES), 0) + start).astype(jnp.float32)
+            choose = jnp.concatenate(
+                [(target == position[t : t + 1, :]).astype(jnp.bfloat16) for t in range(members)],
+                axis=1,
+            )
+            both = jnp.concatenate(
+                [slots_ref[part].reshape(members * ROWS_DEV, LANES) for part in range(2)], axis=1
+            )
+            chosen = jnp.dot(choose, both, preferred_element_type=jnp.float32).astype(jnp.bfloat16)
+            for part in range(2):
+                rows[me, part, pl.ds(start, step), :] = chosen[:, part * LANES : (part + 1) * LANES]
+
+        held = count_ref[pl.ds(lax.axis_index("bucket"), 1), :]
+        place = lax.broadcasted_iota(jnp.int32, (tiles, LANES), 0) * LANES
+        place += lax.broadcasted_iota(jnp.int32, (tiles, LANES), 1)
+        live[...] = (place.astype(jnp.float32) < held).astype(jnp.float32)
+        if sent < capacity:
+            blank = jnp.zeros((capacity - sent, LANES), jnp.bfloat16)
+            for q in range(members):
+                for part in range(2):
+                    rows[q, part, sent:capacity, :] = blank
     pl.semaphore_wait(barrier, members - 1)
 
-    half, quarter = capacity // 2, capacity // 4
-    units = [(0, 0, capacity), (-1, 0, capacity), (1, 0, capacity), (2, 0, half), (2, half, half)]
+    def front(count):
+        return -(-count // 32) * 16
+
+    half = front(sent)
+    units = [(0, 0, sent), (-1, 0, sent), (1, 0, sent), (2, 0, half), (2, half, sent - half)]
     ways = (1, -1)
     pending = {}
 
-    def send(label, part, owner, start, count, neighbour, sems, own=False):
-        source = xs_ref.at[part] if own else rows.at[owner, part]
+    def side(start, count, d):
+        middle = front(count)
+        return (start, middle) if d == 0 else (start + middle, count - middle)
+
+    def send(label, part, owner, span, neighbour, sems):
+        piece = rows.at[owner, part, pl.ds(*span)]
         copy = pltpu.make_async_remote_copy(
-            src_ref=source.at[pl.ds(start, count)],
-            dst_ref=rows.at[owner, part, pl.ds(start, count)],
+            src_ref=piece,
+            dst_ref=piece,
             send_sem=sems[0],
             recv_sem=sems[1],
             device_id={"member": neighbour},
@@ -95,26 +163,25 @@
 
     def first_hop(part, d):
         sems = (first_send.at[part, 0, d], first_recv.at[part, 0, d])
-        send(("f1", part, d), part, me, 0, capacity, member_at(part, ways[d], 0), sems, True)
+        send(("f1", part, d), part, me, (0, sent), member_at(part, ways[d], 0), sems)
 
     def first_forward(part, d):
         sems = (first_send.at[part, 1, d], first_recv.at[part, 1, d])
         owner = member_at(part, -ways[d], 0)
-        send(("f2", part, d), part, owner, d * half, half, member_at(part, ways[d], 0), sems)
+        send(("f2", part, d), part, owner, side(0, sent, d), member_at(part, ways[d], 0), sems)
 
     def second_hop(part, u, d):
         first, start, count = units[u]
         sems = (second_send.at[part, 0, u, d], second_recv.at[part, 0, u, d])
         owner = me if u == 0 else member_at(part, first, 0)
-        send(("g1", part, u, d), part, owner, start, count, member_at(part, 0, ways[d]), sems, u == 0)
+        send(("g1", part, u, d), part, owner, (start, count), member_at(part, 0, ways[d]), sems)
 
     def second_forward(part, u, d):
         first, start, count = units[u]
         sems = (second_send.at[part, 1, u, d], second_recv.at[part, 1, u, d])
         owner = member_at(part, first, -ways[d])
         send(
-            ("g2", part, u, d), part, owner, start + d * (count // 2), count // 2,
-            member_at(part, 0, ways[d]), sems,
+            ("g2", part, u, d), part, owner, side(start, count, d), member_at(part, 0, ways[d]), sems
         )
 
     def arrive(label):
@@ -153,7 +220,6 @@
             noise_rows[q] = block
             wide = block.astype(jnp.float32)
             noise_norm += jnp.sum(wide * wide, axis=1, keepdims=True)
-    own_copy.wait()
     add_slice(me)
 
     for part in range(2):
@@ -243,7 +309,9 @@
         shift = -(peak + jnp.log(total))
         for t in range(tiles):
             lanes = slice(t * LANES, (t + 1) * LANES)
-            row_shift[0:1, lanes] = jnp.where(live_ref[0:1, lanes] > 0.5, shift[t : t + 1, :], -jnp.inf)
+            row_shift[0:1, lanes] = jnp.where(
+                live[t : t + 1, :] > 0.5, shift[t : t + 1, :], -jnp.inf
+            )
         for c in range(noise_count // row_chunk):
             span = slice(c * row_chunk, (c + 1) * row_chunk)
             scores = cost[span, :] + row_shift[0:1, :]
@@ -257,44 +325,35 @@
         for copy in lse_copies:
             copy.wait_send()
 
-    @pl.loop(0, members)
-    def _(q):
-        panel = jnp.concatenate([rows[q, 0], rows[q, 1]], axis=1)
-        start = pl.multiple_of(q * part_width, part_width)
-        out_ref[:, pl.ds(start, part_width)] = jnp.dot(
-            weights[...], panel, preferred_element_type=jnp.float32
-        )
-
-
-def pair(xs, live, noise):
+
+def pair(slots, counts, noise, sent, collective_id):
     members = SIDE * SIDE
-    capacity = xs.shape[1]
+    capacity = -(-sent // (3 * LANES)) * 3 * LANES if sent < members * ROWS_DEV else sent
     noise_count, width = noise.shape
     tiles = capacity // LANES
     part_width = width // members
     dma = pltpu.SemaphoreType.DMA
+    vmem = pl.BlockSpec(memory_space=pltpu.VMEM)
     return pl.pallas_call(
-        functools.partial(pairing_kernel, width),
-        out_shape=jax.ShapeDtypeStruct((noise_count, width), jnp.float32),
-        in_specs=[
-            pl.BlockSpec(memory_space=pltpu.VMEM),
-            pl.BlockSpec(memory_space=pltpu.VMEM),
-            pl.BlockSpec(memory_space=pl.ANY),
-        ],
-        out_specs=pl.BlockSpec(memory_space=pltpu.VMEM),
+        functools.partial(pairing_kernel, width, sent),
+        out_shape=(
+            jax.ShapeDtypeStruct((members, 2, capacity, LANES), jnp.bfloat16),
+            jax.ShapeDtypeStruct((noise_count, capacity), jnp.bfloat16),
+        ),
+        in_specs=[vmem, vmem, pl.BlockSpec(memory_space=pl.ANY)],
+        out_specs=(vmem, vmem),
         scratch_shapes=[
-            pltpu.VMEM((members, 2, capacity, LANES), jnp.bfloat16),
             pltpu.VMEM((noise_count, capacity), jnp.float32),
             pltpu.VMEM((noise_count, width), jnp.float32),
             pltpu.VMEM((members, noise_count, part_width), jnp.bfloat16),
             pltpu.VMEM((8, capacity), jnp.float32),
+            pltpu.VMEM((tiles, LANES), jnp.float32),
+            pltpu.VMEM((members, LANES), jnp.float32),
             pltpu.VMEM((noise_count, LANES), jnp.float32),
             pltpu.VMEM((8, capacity), jnp.float32),
-            pltpu.VMEM((noise_count, capacity), jnp.bfloat16),
             pltpu.VMEM((ITERS, tiles, LANES), jnp.float32),
             pltpu.VMEM((ITERS, members, tiles, LANES), jnp.float32),
             dma((4,)),
-            dma,
             dma((2, 2, 2)),
             dma((2, 2, 2)),
             dma((2, 2, 5, 2)),
@@ -303,33 +362,220 @@
             dma((ITERS, members)),
         ],
         compiler_params=pltpu.CompilerParams(
-            collective_id=0, has_side_effects=True, vmem_limit_bytes=60 * 1024 * 1024
+            collective_id=collective_id, has_side_effects=True, vmem_limit_bytes=30 * 1024 * 1024
         ),
-    )(xs, live, noise)
+    )(slots, counts, noise)
+
+
+def routing_kernel(
+    dest_hbm,
+    loaded_hbm,
+    slots_ref,
+    count_ref,
+    dest_ref,
+    loaded_ref,
+    packed,
+    landed,
+    tally,
+    tally_bucket,
+    tally_member,
+    load_sem,
+    bucket_send,
+    bucket_recv,
+    member_send,
+    member_recv,
+    tally_send,
+    tally_recv,
+):
+    groups, members = BUCKETS, SIDE * SIDE
+    loaded, width = loaded_ref.shape
+    part_width = width // members
+    block = ROWS_DEV // groups
+    my_bucket, me = lax.axis_index("bucket"), lax.axis_index("member")
+    bucket_peers = [(my_bucket + k) % groups for k in range(groups)]
+    member_peers = [(me + k) % members for k in range(members)]
+
+    dest_copy = pltpu.make_async_copy(dest_hbm, dest_ref, load_sem.at[0])
+    dest_copy.start()
+    load_copy = pltpu.make_async_copy(loaded_hbm, loaded_ref, load_sem.at[1])
+    load_copy.start()
+    barrier = pltpu.get_barrier_semaphore()
+    for peer in bucket_peers[1:]:
+        pl.semaphore_signal(barrier, inc=1, device_id={"bucket": peer}, device_id_type=MESH)
+    for peer in member_peers[1:]:
+        pl.semaphore_signal(barrier, inc=1, device_id={"member": peer}, device_id_type=MESH)
+
+    dest_copy.wait()
+    dest = dest_ref[...]
+    hits = (lax.broadcasted_iota(jnp.int32, (groups, loaded), 0) == dest).astype(jnp.float32)
+    up_to = (
+        lax.broadcasted_iota(jnp.int32, (loaded, loaded), 0)
+        <= lax.broadcasted_iota(jnp.int32, (loaded, loaded), 1)
+    ).astype(jnp.bfloat16)
+    ranks = jnp.dot(hits.astype(jnp.bfloat16), up_to, preferred_element_type=jnp.float32)
+    place = jnp.sum(hits * (ranks - 1.0), axis=0, keepdims=True).astype(jnp.int32) + dest * block
+    pick = lax.broadcasted_iota(jnp.int32, (ROWS_DEV, loaded), 0) == place
+    pick = pick.astype(jnp.float32)
+    fill = EMPTY * (1.0 - jnp.sum(pick, axis=1, keepdims=True))
+    pick = pick.astype(jnp.bfloat16)
+    tally[0] = jnp.broadcast_to(jnp.sum(hits, axis=1, keepdims=True), tally.shape[1:])
+    load_copy.wait()
+
+    def pack(k):
+        start = pl.multiple_of(member_peers[k] * part_width, part_width)
+        panel = loaded_ref[:, pl.ds(start, part_width)].astype(jnp.bfloat16)
+        sorted_panel = jnp.dot(pick, panel, preferred_element_type=jnp.float32) + fill
+        sorted_panel = sorted_panel.astype(jnp.bfloat16)
+        for part in range(2):
+            packed[part, k] = sorted_panel[:, part * LANES : (part + 1) * LANES]
+
+    def block_of(bucket):
+        return pl.ds(pl.multiple_of(bucket * block, block), block)
+
+    def to_bucket(stage, k, source, target):
+        copy = pltpu.make_async_remote_copy(
+            src_ref=source.at[:, block_of(bucket_peers[k])],
+            dst_ref=target.at[:, block_of(my_bucket)],
+            send_sem=bucket_send.at[stage, k],
+            recv_sem=bucket_recv.at[stage, k],
+            device_id={"bucket": bucket_peers[k]},
+            device_id_type=MESH,
+        )
+        copy.start()
+        return copy
+
+    def to_member(stage, k, source, target):
+        copy = pltpu.make_async_remote_copy(
+            src_ref=source,
+            dst_ref=target,
+            send_sem=member_send.at[stage, k],
+            recv_sem=member_recv.at[stage, k],
+            device_id={"member": member_peers[k]},
+            device_id_type=MESH,
+        )
+        copy.start()
+        return copy
+
+    def tell(stage, k, target, axis, peer):
+        copy = pltpu.make_async_remote_copy(
+            src_ref=tally.at[stage],
+            dst_ref=target.at[k],
+            send_sem=tally_send.at[stage, k],
+            recv_sem=tally_recv.at[stage, k],
+            device_id={axis: peer},
+            device_id_type=MESH,
+        )
+        copy.start()
+        return copy
+
+    for k in range(members):
+        pack(k)
+    pl.semaphore_wait(barrier, groups + members - 2)
+    bucket_tally = [tell(0, k, tally_bucket, "bucket", bucket_peers[k]) for k in range(1, groups)]
+    first_bucket, first_member = [], []
+    for k in range(1, members):
+        if k < groups:
+            first_bucket.append(to_bucket(0, k, packed.at[0], landed.at[0]))
+        first_member.append(to_member(0, k, packed.at[1, k], landed.at[1, me]))
+    landed[0, :, block_of(my_bucket), :] = packed[0, :, block_of(my_bucket), :]
+    landed[1, me] = packed[1, 0]
+
+    for copy in first_bucket:
+        copy.wait_recv()
+    second_member = [
+        to_member(1, k, landed.at[0, k], slots_ref.at[0, me]) for k in range(1, members)
+    ]
+    slots_ref[0, me] = landed[0, 0]
+    for copy in first_member:
+        copy.wait_recv()
+    second_bucket = [to_bucket(1, k, landed.at[1], slots_ref.at[1]) for k in range(1, groups)]
+    slots_ref[1, :, block_of(my_bucket), :] = landed[1, :, block_of(my_bucket), :]
+
+    total = tally[0]
+    for k in range(1, groups):
+        bucket_tally[k - 1].wait_recv()
+        total += tally_bucket[k]
+    tally[1] = total
+    member_tally = [tell(1, k, tally_member, "member", member_peers[k]) for k in range(1, members)]
+    for k in range(1, members):
+        member_tally[k - 1].wait_recv()
+        total += tally_member[k]
+    count_ref[...] = total
+    for copy in second_member + second_bucket:
+        copy.wait_recv()
+    for copy in (
+        first_bucket + first_member + second_member + second_bucket + bucket_tally + member_tally
+    ):
+        copy.wait_send()
+
+
+def route(dest_bucket, loader_rows):
+    members = SIDE * SIDE
+    loaded, width = loader_rows.shape
+    dma = pltpu.SemaphoreType.DMA
+    vmem = pl.BlockSpec(memory_space=pltpu.VMEM)
+    anywhere = pl.BlockSpec(memory_space=pl.ANY)
+    return pl.pallas_call(
+        routing_kernel,
+        out_shape=(
+            jax.ShapeDtypeStruct((2, members, ROWS_DEV, LANES), jnp.bfloat16),
+            jax.ShapeDtypeStruct((BUCKETS, LANES), jnp.float32),
+        ),
+        in_specs=[anywhere, anywhere],
+        out_specs=(vmem, vmem),
+        scratch_shapes=[
+            pltpu.VMEM((1, loaded), jnp.int32),
+            pltpu.VMEM((loaded, width), jnp.float32),
+            pltpu.VMEM((2, members, ROWS_DEV, LANES), jnp.bfloat16),
+            pltpu.VMEM((2, members, ROWS_DEV, LANES), jnp.bfloat16),
+            pltpu.VMEM((2, BUCKETS, LANES), jnp.float32),
+            pltpu.VMEM((BUCKETS, BUCKETS, LANES), jnp.float32),
+            pltpu.VMEM((members, BUCKETS, LANES), jnp.float32),
+            dma((2,)),
+            dma((2, BUCKETS)),
+            dma((2, BUCKETS)),
+            dma((2, members)),
+            dma((2, members)),
+            dma((2, members)),
+            dma((2, members)),
+        ],
+        compiler_params=pltpu.CompilerParams(
+            collective_id=1, has_side_effects=True, vmem_limit_bytes=16 * 1024 * 1024
+        ),
+    )(dest_bucket.reshape(1, -1), loader_rows)
+
+
+def targets_kernel(rows_ref, weights_ref, out_ref):
+    q = pl.program_id(0)
+    panel = jnp.concatenate([rows_ref[q, 0], rows_ref[q, 1]], axis=1)
+    out_ref[...] = jnp.dot(weights_ref[...], panel, preferred_element_type=jnp.float32)
+
+
+def multiply(rows, weights):
+    members, _, capacity, _ = rows.shape
+    noise_count = weights.shape[0]
+    width = members * 2 * LANES
+    vmem = pl.BlockSpec(memory_space=pltpu.VMEM)
+    return pl.pallas_call(
+        targets_kernel,
+        out_shape=jax.ShapeDtypeStruct((noise_count, width), jnp.float32),
+        grid=(members,),
+        in_specs=[vmem, vmem],
+        out_specs=pl.BlockSpec((noise_count, 2 * LANES), lambda q: (0, q)),
+        compiler_params=pltpu.CompilerParams(vmem_limit_bytes=24 * 1024 * 1024),
+    )(rows, weights)
 
 
 def body(loader_rows, dest_bucket, dest_slot, noise):
-    groups = lax.axis_size("bucket")
-    members = lax.axis_size("member")
-    loaded, width = loader_rows.shape
-    capacity = ROWS_DEV // groups
-    rounded = loader_rows.astype(jnp.bfloat16)
-    index = jnp.arange(loaded, dtype=jnp.int32)
-    earlier = (dest_bucket[:, None] == dest_bucket[None, :]) & (index[None, :] < index[:, None])
-    position = dest_bucket * capacity + jnp.sum(earlier.astype(jnp.int32), axis=1)
-    hits = position[None, :] == jnp.arange(groups * capacity, dtype=jnp.int32)[:, None]
-    packed = jnp.dot(hits.astype(jnp.bfloat16), rounded, preferred_element_type=jnp.float32)
-    filled = jnp.any(hits, axis=1)
-    packed = jnp.where(filled[:, None], packed, EMPTY).astype(jnp.bfloat16)
-    packed = packed.reshape(groups, capacity, members, width // members)
-    packed = packed.transpose(0, 2, 1, 3).reshape(groups * members, capacity, width // members)
-    got = lax.all_to_all(packed, ("bucket", "member"), split_axis=0, concat_axis=0, tiled=True)
-    got = got.reshape(groups * members * capacity, width // members)
-    live = got[:, 0] < 0.5 * EMPTY
-    got = jnp.where(live[:, None], got, jnp.zeros_like(got))
-    xs = jnp.stack([got[:, :LANES], got[:, LANES:]])
-    live_rows = jnp.broadcast_to(live.astype(jnp.float32)[None, :], (8, live.shape[0]))
-    return pair(xs, live_rows, noise)
+    slots, counts = route(dest_bucket, loader_rows)
+
+    def all_slots(slots, counts, noise):
+        return multiply(*pair(slots, counts, noise, slots.shape[1] * ROWS_DEV, 2))
+
+    def live_first(slots, counts, noise):
+        return multiply(*pair(slots, counts, noise, FAST_ROWS, 0))
+
+    return lax.cond(jnp.all(counts <= FAST_ROWS), live_first, all_slots, slots, counts, noise)
 
 
 def solution(mesh):

time: 169 us -> 115 us (0.68)
  blocking collectives: 30 us -> 0 us
  Pallas kernels: 128 us -> 109 us
  other arithmetic: 3.63 us -> 0.63 us
  local copies, waits for them, and re-layouts: 6.07 us -> 3.89 us
  matrix products: 1.77 us -> 0 us
    all_to_all x1 -> x0, blocking collectives: 30 us -> none  [body(): lax.all_to_all(packed, ('bucket', 'member'), split_axis=0, concat_axis=0,...]
    pallas_call x1 -> x3, Pallas kernels: 128 us -> 109 us  [the longest x1 76.3 us: pair(): pl.pallas_call(functools.partial(pairing_kernel, width, sent), out_shape=...]
    dot_general x1 -> x0, matrix products: 1.77 us -> none  [body(): jnp.dot(hits.astype(jnp.bfloat16), rounded, preferred_element_type=jnp.fl...]
    unnamed x2 -> x6, local copies, waits for them, and re-layouts: 4.9 us -> 3.89 us
where the time goes in v3:
time: 115 us
  Pallas kernels  109 us (95%)
  local copies, waits for them, and re-layouts  3.89 us (3%)
    pallas_call x1, Pallas kernels, pair(): pl.pallas_call(functools.partial(pairing_kernel, width, sent), out_shape=...  76.3 us
    pallas_call x1, Pallas kernels, route(): pl.pallas_call(routing_kernel, out_shape=(jax.ShapeDtypeStruct((2, member...  27.4 us
    pallas_call x1, Pallas kernels, multiply(): pl.pallas_call(targets_kernel, out_shape=jax.ShapeDtypeStruct((noise_coun...  5.64 us
    unnamed x6, local copies, waits for them, and re-layouts  3.89 us

profile of v3, /device:TPU:0, one launch (start us, length us, event | category | flops | bytes accessed | tf_op | source)
XLA Modules:
  0.0 114.8 jit_solution(9260517731843280463)
XLA Ops:
  0.0 0.0 copy-start
  0.0 1.2 %copy-done = f32[64,4096]{1,0:T(8,128)S(1)} copy-done((f32[64,4096]{1,0:T(8,128)S(1)}, f32[64,4096]{1,0:T(8,128)}, u32[]{:S(2)}) %copy-start) | copy-done | bytes 1048600
  1.2 0.0 copy-start.1
  1.2 0.7 copy-done.1
  1.9 27.4 %shard_map.39 = (bf16[2,16,128,128]{3,2,1,0:T(8,128)(2,1)S(1)}, f32[8,128]{1,0:T(8,128)S(1)}) custom-call(s32[1,64]{1,0:T(1,128)S(1)} %bitcast.1, f32[64,4096]{1,0:T(8,128)S(1)} %copy-done), custom_call_target="tpu_custom_call" | custom-call | tf_op jit(solution)/shard_map/pallas_call | solution.py:518
  29.3 0.6 compare_reduce_fusion
  30.6 82.1 %conditional.1 = (f32[256,4096]{1,0:T(8,128)S(1)}) conditional(s32[]{:T(128)} %convert_element_type.3, (bf16[2,16,128,128]{3,2,1,0:T(8,128)(2,1)S(1)}, f32[8,128]{1,0:T(8,128)S(1)}, f32[256,4096]{1,0:T(8,128)}) %tuple.11, (bf16[2,16,128,128]{3,2,1,0:T(8,128)(2,1)S(1)}, f32[8,128]{1,0:T(8,128)S(1)}, f32[256,4096]{1,0:T(8,128)}) %tuple.11), branch_computations={%region_1.0_spmd, %region_2.0_spmd} | conditional | bytes 8 | solution.py:578
  30.8 76.3 %branch_1_fun.2 = (bf16[16,2,1152,128]{3,2,1,0:T(8,128)(2,1)S(1)}, bf16[256,1152]{1,0:T(8,128)(2,1)S(1)}) custom-call(bf16[2,16,128,128]{3,2,1,0:T(8,128)(2,1)S(1)} %get-tuple-element.25.slots_ref, f32[8,128]{1,0:T(8,128)S(1)} %get-tuple-element.26.count_ref, f32[256,4096]{1,0:T(8,128)} %get-tuple-element.27.noise_ref), custom_call_target="tpu_custom_call" | custom-call | tf_op jit(solution)/shard_map/cond/branch_1_fun/pallas_call | solution.py:337
  107.1 5.6 %branch_1_fun.3 = f32[256,4096]{1,0:T(8,128)S(1)} custom-call(bf16[16,2,1152,128]{3,2,1,0:T(8,128)(2,1)S(1)} %get-tuple-element.28.rows_ref, bf16[256,1152]{1,0:T(8,128)(2,1)S(1)} %get-tuple-element.29.weights_ref), custom_call_target="tpu_custom_call" | custom-call | tf_op jit(solution)/shard_map/cond/branch_1_fun/pallas_call | solution.py:559
  112.7 0.0 copy-start.2
  112.8 2.0 %copy-done.2 = f32[256,4096]{1,0:T(8,128)} copy-done((f32[256,4096]{1,0:T(8,128)}, f32[256,4096]{1,0:T(8,128)S(1)}, u32[]{:S(2)}) %copy-start.2) | copy-done | bytes 4194328
Async XLA Ops:
  0.0 1.2 %copy-start = (f32[64,4096]{1,0:T(8,128)S(1)}, f32[64,4096]{1,0:T(8,128)}, u32[]{:S(2)}) copy-start(f32[64,4096]{1,0:T(8,128)} %loaded_hbm.1) | copy-start | bytes 3145732
  1.2 0.7 copy-start.1
  112.7 2.0 %copy-start.2 = (f32[256,4096]{1,0:T(8,128)}, f32[256,4096]{1,0:T(8,128)S(1)}, u32[]{:S(2)}) copy-start(f32[256,4096]{1,0:T(8,128)S(1)} %get-tuple-element.37) | copy-start | bytes 12582916

commit v4 on v3

--- a/solution.py
+++ b/solution.py
@@ -19,36 +19,12 @@
 CONTRACT_LAST = (((1,), (1,)), ((), ()))
 
 
-def pairing_kernel(
-    width,
-    sent,
-    slots_ref,
-    count_ref,
-    noise_ref,
-    rows,
-    weights,
-    cost,
-    noise_wide,
-    noise_rows,
-    row_norm,
-    live,
-    position,
-    col_shift,
-    row_shift,
-    lse_out,
-    lse_in,
-    noise_sem,
-    first_send,
-    first_recv,
-    second_send,
-    second_recv,
-    lse_send,
-    lse_recv,
-):
+def solve(width, sent, eager, prepare, extra, noise_norm_of, rows, weights, scratch):
+    (cost, noise_rows, row_norm, live, col_shift, row_shift, lse_out, lse_in,
+     first_send, first_recv, second_send, second_recv, lse_send, lse_recv) = scratch
     members = SIDE * SIDE
     capacity = rows.shape[2]
-    noise_count = noise_wide.shape[0]
-    part_width = width // members
+    noise_count = cost.shape[0]
     tiles = capacity // LANES
     scale = 1.0 / (width * (0.64 / math.sqrt(width)))
     me = lax.axis_index("member")
@@ -57,84 +33,6 @@
     def member_at(part, first, second):
         along_x, along_z = (first, second) if part == 0 else (second, first)
         return ((my_z + along_z + SIDE) % SIDE) * SIDE + (my_x + along_x + SIDE) % SIDE
-
-    chunk = width // 4
-    noise_copies = []
-    for k in range(4):
-        copy = pltpu.make_async_copy(
-            noise_ref.at[:, pl.ds(k * chunk, chunk)],
-            noise_wide.at[:, pl.ds(k * chunk, chunk)],
-            noise_sem.at[k],
-        )
-        copy.start()
-        noise_copies.append(copy)
-
-    barrier = pltpu.get_barrier_semaphore()
-    for k in range(1, members):
-        pl.semaphore_signal(
-            barrier, inc=1, device_id={"member": (me + k) % members}, device_id_type=MESH
-        )
-
-    marks = jnp.concatenate(
-        [
-            lax.dot_general(
-                jnp.ones((8, LANES), jnp.bfloat16), slots_ref[0, t], CONTRACT_LAST,
-                preferred_element_type=jnp.float32,
-            )[0:1]
-            for t in range(members)
-        ],
-        axis=0,
-    )
-    alive = (marks < 0.5 * LANES * EMPTY).astype(jnp.float32)
-    if capacity == members * ROWS_DEV:
-        live[...] = alive
-        for part in range(2):
-            for t in range(members):
-                block = slots_ref[part, t].astype(jnp.float32)
-                block = jnp.where(block < 0.5 * EMPTY, block, 0.0)
-                rows[me, part, t * ROWS_DEV : (t + 1) * ROWS_DEV, :] = block.astype(jnp.bfloat16)
-    else:
-        before = (
-            lax.broadcasted_iota(jnp.int32, (LANES, LANES), 0)
-            <= lax.broadcasted_iota(jnp.int32, (LANES, LANES), 1)
-        ).astype(jnp.bfloat16)
-        inside = jnp.dot(alive.astype(jnp.bfloat16), before, preferred_element_type=jnp.float32)
-        per_member = jnp.broadcast_to(inside[:, LANES - 1 : LANES], (members, LANES))
-        earlier = (
-            lax.broadcasted_iota(jnp.int32, (members, members), 0)
-            > lax.broadcasted_iota(jnp.int32, (members, members), 1)
-        ).astype(jnp.bfloat16)
-        offset = jnp.dot(
-            earlier, per_member.astype(jnp.bfloat16), preferred_element_type=jnp.float32
-        )
-        position[...] = jnp.where(alive > 0.5, inside + offset - 1.0, -1.0)
-        step = capacity // 3
-
-        @pl.loop(0, 3)
-        def _(c):
-            start = pl.multiple_of(c * step, LANES)
-            target = (lax.broadcasted_iota(jnp.int32, (step, LANES), 0) + start).astype(jnp.float32)
-            choose = jnp.concatenate(
-                [(target == position[t : t + 1, :]).astype(jnp.bfloat16) for t in range(members)],
-                axis=1,
-            )
-            both = jnp.concatenate(
-                [slots_ref[part].reshape(members * ROWS_DEV, LANES) for part in range(2)], axis=1
-            )
-            chosen = jnp.dot(choose, both, preferred_element_type=jnp.float32).astype(jnp.bfloat16)
-            for part in range(2):
-                rows[me, part, pl.ds(start, step), :] = chosen[:, part * LANES : (part + 1) * LANES]
-
-        held = count_ref[pl.ds(lax.axis_index("bucket"), 1), :]
-        place = lax.broadcasted_iota(jnp.int32, (tiles, LANES), 0) * LANES
-        place += lax.broadcasted_iota(jnp.int32, (tiles, LANES), 1)
-        live[...] = (place.astype(jnp.float32) < held).astype(jnp.float32)
-        if sent < capacity:
-            blank = jnp.zeros((capacity - sent, LANES), jnp.bfloat16)
-            for q in range(members):
-                for part in range(2):
-                    rows[q, part, sent:capacity, :] = blank
-    pl.semaphore_wait(barrier, members - 1)
 
     def front(count):
         return -(-count // 32) * 16
@@ -188,6 +86,10 @@
         pending[label].wait_recv()
 
     def add_slice(owner):
+        if eager:
+            add_panel(owner)
+
+    def add_panel(owner):
         panel = jnp.concatenate([rows[owner, 0], rows[owner, 1]], axis=1)
         cost[...] += lax.dot_general(
             noise_rows[owner], panel, CONTRACT_LAST, preferred_element_type=jnp.float32
@@ -202,24 +104,15 @@
         ) + lax.dot_general(ones, low, CONTRACT_LAST, preferred_element_type=jnp.float32)
 
     for part in range(2):
+        prepare(part)
         for d in range(2):
             first_hop(part, d)
-    for part in range(2):
         for d in range(2):
             second_hop(part, 0, d)
-
+    extra()
     cost[...] = jnp.zeros_like(cost)
     row_norm[...] = jnp.zeros_like(row_norm)
-    per_chunk = chunk // part_width
-    noise_norm = jnp.zeros((noise_count, 1), jnp.float32)
-    for k in range(4):
-        noise_copies[k].wait()
-        for s in range(per_chunk):
-            q = k * per_chunk + s
-            block = noise_wide[:, q * part_width : (q + 1) * part_width].astype(jnp.bfloat16)
-            noise_rows[q] = block
-            wide = block.astype(jnp.float32)
-            noise_norm += jnp.sum(wide * wide, axis=1, keepdims=True)
+    noise_norm = noise_norm_of()
     add_slice(me)
 
     for part in range(2):
@@ -273,6 +166,9 @@
     for copy in pending.values():
         copy.wait_send()
 
+    if not eager:
+        pl.loop(0, members)(add_panel)
+
     for t in range(tiles):
         lanes = slice(t * LANES, (t + 1) * LANES)
         cost[:, lanes] = (2.0 * cost[:, lanes] - row_norm[0:1, lanes] - noise_norm) * scale
@@ -326,50 +222,79 @@
             copy.wait_send()
 
 
-def pair(slots, counts, noise, sent, collective_id):
+def start_noise(noise_hbm, noise_wide, noise_sem):
+    chunk = noise_wide.shape[1] // 4
+    copies = []
+    for k in range(4):
+        columns = pl.ds(k * chunk, chunk)
+        copy = pltpu.make_async_copy(
+            noise_hbm.at[:, columns], noise_wide.at[:, columns], noise_sem.at[k]
+        )
+        copy.start()
+        copies.append(copy)
+    return copies
+
+
+def round_noise(copies, noise_wide, noise_rows):
+    noise_count, part_width = noise_rows.shape[1:]
+    per_chunk = noise_rows.shape[0] // 4
+    noise_norm = jnp.zeros((noise_count, 1), jnp.float32)
+    for k in range(4):
+        copies[k].wait()
+        for s in range(per_chunk):
+            q = k * per_chunk + s
+            block = noise_wide[:, q * part_width : (q + 1) * part_width].astype(jnp.bfloat16)
+            noise_rows[q] = block
+            wide = block.astype(jnp.float32)
+            noise_norm += jnp.sum(wide * wide, axis=1, keepdims=True)
+    return noise_norm
+
+
+def marked_live(slots_ref):
+    marks = jnp.concatenate(
+        [
+            lax.dot_general(
+                jnp.ones((8, LANES), jnp.bfloat16), slots_ref[0, t], CONTRACT_LAST,
+                preferred_element_type=jnp.float32,
+            )[0:1]
+            for t in range(slots_ref.shape[1])
+        ],
+        axis=0,
+    )
+    return (marks < 0.5 * LANES * EMPTY).astype(jnp.float32)
+
+
+def all_slots_kernel(width, slots_ref, noise_hbm, rows, weights, noise_wide, noise_sem, *scratch):
+    noise_rows, live = scratch[1], scratch[3]
     members = SIDE * SIDE
-    capacity = -(-sent // (3 * LANES)) * 3 * LANES if sent < members * ROWS_DEV else sent
-    noise_count, width = noise.shape
-    tiles = capacity // LANES
-    part_width = width // members
-    dma = pltpu.SemaphoreType.DMA
-    vmem = pl.BlockSpec(memory_space=pltpu.VMEM)
-    return pl.pallas_call(
-        functools.partial(pairing_kernel, width, sent),
-        out_shape=(
-            jax.ShapeDtypeStruct((members, 2, capacity, LANES), jnp.bfloat16),
-            jax.ShapeDtypeStruct((noise_count, capacity), jnp.bfloat16),
-        ),
-        in_specs=[vmem, vmem, pl.BlockSpec(memory_space=pl.ANY)],
-        out_specs=(vmem, vmem),
-        scratch_shapes=[
-            pltpu.VMEM((noise_count, capacity), jnp.float32),
-            pltpu.VMEM((noise_count, width), jnp.float32),
-            pltpu.VMEM((members, noise_count, part_width), jnp.bfloat16),
-            pltpu.VMEM((8, capacity), jnp.float32),
-            pltpu.VMEM((tiles, LANES), jnp.float32),
-            pltpu.VMEM((members, LANES), jnp.float32),
-            pltpu.VMEM((noise_count, LANES), jnp.float32),
-            pltpu.VMEM((8, capacity), jnp.float32),
-            pltpu.VMEM((ITERS, tiles, LANES), jnp.float32),
-            pltpu.VMEM((ITERS, members, tiles, LANES), jnp.float32),
-            dma((4,)),
-            dma((2, 2, 2)),
-            dma((2, 2, 2)),
-            dma((2, 2, 5, 2)),
-            dma((2, 2, 5, 2)),
-            dma((ITERS, members)),
-            dma((ITERS, members)),
-        ],
-        compiler_params=pltpu.CompilerParams(
-            collective_id=collective_id, has_side_effects=True, vmem_limit_bytes=30 * 1024 * 1024
-        ),
-    )(slots, counts, noise)
-
-
-def routing_kernel(
+    me = lax.axis_index("member")
+    noise_copies = start_noise(noise_hbm, noise_wide, noise_sem)
+    barrier = pltpu.get_barrier_semaphore()
+    for k in range(1, members):
+        pl.semaphore_signal(
+            barrier, inc=1, device_id={"member": (me + k) % members}, device_id_type=MESH
+        )
+    live[...] = marked_live(slots_ref)
+    for part in range(2):
+        for t in range(members):
+            block = slots_ref[part, t].astype(jnp.float32)
+            block = jnp.where(block < 0.5 * EMPTY, block, 0.0)
+            rows[me, part, t * ROWS_DEV : (t + 1) * ROWS_DEV, :] = block.astype(jnp.bfloat16)
+    pl.semaphore_wait(barrier, members - 1)
+    solve(
+        width, rows.shape[2], False, lambda part: None, lambda: None,
+        lambda: round_noise(noise_copies, noise_wide, noise_rows), rows, weights, scratch,
+    )
+
+
+def live_rows_kernel(
+    width,
+    sent,
     dest_hbm,
     loaded_hbm,
+    noise_hbm,
+    rows,
+    weights,
     slots_ref,
     count_ref,
     dest_ref,
@@ -386,9 +311,17 @@
     member_recv,
     tally_send,
     tally_recv,
+    position,
+    choose,
+    noise_wide,
+    noise_sem,
+    *scratch,
 ):
+    noise_rows, live = scratch[1], scratch[3]
     groups, members = BUCKETS, SIDE * SIDE
-    loaded, width = loaded_ref.shape
+    loaded = loaded_ref.shape[0]
+    capacity = rows.shape[2]
+    tiles = capacity // LANES
     part_width = width // members
     block = ROWS_DEV // groups
     my_bucket, me = lax.axis_index("bucket"), lax.axis_index("member")
@@ -399,6 +332,7 @@
     dest_copy.start()
     load_copy = pltpu.make_async_copy(loaded_hbm, loaded_ref, load_sem.at[1])
     load_copy.start()
+    noise_copies = start_noise(noise_hbm, noise_wide, noise_sem)
     barrier = pltpu.get_barrier_semaphore()
     for peer in bucket_peers[1:]:
         pl.semaphore_signal(barrier, inc=1, device_id={"bucket": peer}, device_id_type=MESH)
@@ -480,6 +414,13 @@
     landed[0, :, block_of(my_bucket), :] = packed[0, :, block_of(my_bucket), :]
     landed[1, me] = packed[1, 0]
 
+    noise_norm = round_noise(noise_copies, noise_wide, noise_rows)
+    if sent < capacity:
+        blank = jnp.zeros((capacity - sent, LANES), jnp.bfloat16)
+        for q in range(members):
+            for part in range(2):
+                rows[q, part, sent:capacity, :] = blank
+
     for copy in first_bucket:
         copy.wait_recv()
     second_member = [
@@ -490,39 +431,121 @@
         copy.wait_recv()
     second_bucket = [to_bucket(1, k, landed.at[1], slots_ref.at[1]) for k in range(1, groups)]
     slots_ref[1, :, block_of(my_bucket), :] = landed[1, :, block_of(my_bucket), :]
-
     total = tally[0]
     for k in range(1, groups):
         bucket_tally[k - 1].wait_recv()
         total += tally_bucket[k]
     tally[1] = total
     member_tally = [tell(1, k, tally_member, "member", member_peers[k]) for k in range(1, members)]
-    for k in range(1, members):
-        member_tally[k - 1].wait_recv()
-        total += tally_member[k]
-    count_ref[...] = total
-    for copy in second_member + second_bucket:
-        copy.wait_recv()
+
+    def find_positions():
+        alive = marked_live(slots_ref)
+        before = (
+            lax.broadcasted_iota(jnp.int32, (LANES, LANES), 0)
+            <= lax.broadcasted_iota(jnp.int32, (LANES, LANES), 1)
+        ).astype(jnp.bfloat16)
+        inside = jnp.dot(alive.astype(jnp.bfloat16), before, preferred_element_type=jnp.float32)
+        per_member = jnp.broadcast_to(inside[:, LANES - 1 : LANES], (members, LANES))
+        earlier = (
+            lax.broadcasted_iota(jnp.int32, (members, members), 0)
+            > lax.broadcasted_iota(jnp.int32, (members, members), 1)
+        ).astype(jnp.bfloat16)
+        offset = jnp.dot(
+            earlier, per_member.astype(jnp.bfloat16), preferred_element_type=jnp.float32
+        )
+        position[...] = jnp.where(alive > 0.5, inside + offset - 1.0, -1.0)
+        held = jnp.sum(per_member, axis=0, keepdims=True)
+        place = lax.broadcasted_iota(jnp.int32, (tiles, LANES), 0) * LANES
+        place += lax.broadcasted_iota(jnp.int32, (tiles, LANES), 1)
+        live[...] = (place.astype(jnp.float32) < held).astype(jnp.float32)
+
+    step = capacity // 3
+
+    def prepare(part):
+        for copy in second_bucket if part else second_member:
+            copy.wait_recv()
+        if part == 0:
+            find_positions()
+
+        @pl.loop(0, 3)
+        def _(c):
+            start = pl.multiple_of(c * step, LANES)
+            span = pl.ds(start, step)
+            if part == 0:
+                target = lax.broadcasted_iota(jnp.int32, (step, LANES), 0) + start
+                target = target.astype(jnp.float32)
+                for t in range(members):
+                    choose[span, t * LANES : (t + 1) * LANES] = (
+                        target == position[t : t + 1, :]
+                    ).astype(jnp.bfloat16)
+            rows[me, part, span, :] = jnp.dot(
+                choose[span, :],
+                slots_ref[part].reshape(members * ROWS_DEV, LANES),
+                preferred_element_type=jnp.float32,
+            ).astype(jnp.bfloat16)
+
+    def finish_count():
+        total = tally[1]
+        for k in range(1, members):
+            member_tally[k - 1].wait_recv()
+            total += tally_member[k]
+        count_ref[...] = total
+
+    solve(width, sent, True, prepare, finish_count, lambda: noise_norm, rows, weights, scratch)
     for copy in (
         first_bucket + first_member + second_member + second_bucket + bucket_tally + member_tally
     ):
         copy.wait_send()
 
 
-def route(dest_bucket, loader_rows):
+def solve_scratch(noise_count, capacity, width):
     members = SIDE * SIDE
+    tiles = capacity // LANES
+    dma = pltpu.SemaphoreType.DMA
+    return [
+        pltpu.VMEM((noise_count, width), jnp.float32),
+        dma((4,)),
+        pltpu.VMEM((noise_count, capacity), jnp.float32),
+        pltpu.VMEM((members, noise_count, width // members), jnp.bfloat16),
+        pltpu.VMEM((8, capacity), jnp.float32),
+        pltpu.VMEM((tiles, LANES), jnp.float32),
+        pltpu.VMEM((noise_count, LANES), jnp.float32),
+        pltpu.VMEM((8, capacity), jnp.float32),
+        pltpu.VMEM((ITERS, tiles, LANES), jnp.float32),
+        pltpu.VMEM((ITERS, members, tiles, LANES), jnp.float32),
+        dma((2, 2, 2)),
+        dma((2, 2, 2)),
+        dma((2, 2, 5, 2)),
+        dma((2, 2, 5, 2)),
+        dma((ITERS, members)),
+        dma((ITERS, members)),
+    ]
+
+
+IN_VMEM = pl.BlockSpec(memory_space=pltpu.VMEM)
+IN_HBM = pl.BlockSpec(memory_space=pltpu.HBM)
+
+
+def in_hbm(array):
+    return pltpu.with_memory_space_constraint(array, pltpu.HBM)
+
+
+def pair_live_rows(dest_bucket, loader_rows, noise):
+    members = SIDE * SIDE
+    capacity = -(-FAST_ROWS // (3 * LANES)) * 3 * LANES
     loaded, width = loader_rows.shape
+    noise_count = noise.shape[0]
     dma = pltpu.SemaphoreType.DMA
-    vmem = pl.BlockSpec(memory_space=pltpu.VMEM)
-    anywhere = pl.BlockSpec(memory_space=pl.ANY)
     return pl.pallas_call(
-        routing_kernel,
+        functools.partial(live_rows_kernel, width, FAST_ROWS),
         out_shape=(
+            jax.ShapeDtypeStruct((members, 2, capacity, LANES), jnp.bfloat16),
+            jax.ShapeDtypeStruct((noise_count, capacity), jnp.bfloat16),
             jax.ShapeDtypeStruct((2, members, ROWS_DEV, LANES), jnp.bfloat16),
             jax.ShapeDtypeStruct((BUCKETS, LANES), jnp.float32),
         ),
-        in_specs=[anywhere, anywhere],
-        out_specs=(vmem, vmem),
+        in_specs=[IN_HBM, IN_HBM, IN_HBM],
+        out_specs=(IN_VMEM, IN_VMEM, IN_VMEM, IN_VMEM),
         scratch_shapes=[
             pltpu.VMEM((1, loaded), jnp.int32),
             pltpu.VMEM((loaded, width), jnp.float32),
@@ -538,44 +561,83 @@
             dma((2, members)),
             dma((2, members)),
             dma((2, members)),
+            pltpu.VMEM((members, LANES), jnp.float32),
+            pltpu.VMEM((capacity, members * ROWS_DEV), jnp.bfloat16),
+            *solve_scratch(noise_count, capacity, width),
         ],
         compiler_params=pltpu.CompilerParams(
-            collective_id=1, has_side_effects=True, vmem_limit_bytes=16 * 1024 * 1024
+            collective_id=0, has_side_effects=True, vmem_limit_bytes=20 * 1024 * 1024
         ),
-    )(dest_bucket.reshape(1, -1), loader_rows)
-
-
-def targets_kernel(rows_ref, weights_ref, out_ref):
-    q = pl.program_id(0)
-    panel = jnp.concatenate([rows_ref[q, 0], rows_ref[q, 1]], axis=1)
-    out_ref[...] = jnp.dot(weights_ref[...], panel, preferred_element_type=jnp.float32)
+    )(*[in_hbm(array) for array in (dest_bucket.reshape(1, -1), loader_rows, noise)])
+
+
+def pair_all_slots(slots, noise):
+    members = SIDE * SIDE
+    capacity = members * ROWS_DEV
+    noise_count, width = noise.shape
+    return pl.pallas_call(
+        functools.partial(all_slots_kernel, width),
+        out_shape=(
+            jax.ShapeDtypeStruct((members, 2, capacity, LANES), jnp.bfloat16),
+            jax.ShapeDtypeStruct((noise_count, capacity), jnp.bfloat16),
+        ),
+        in_specs=[IN_VMEM, IN_HBM],
+        out_specs=(IN_VMEM, IN_VMEM),
+        scratch_shapes=solve_scratch(noise_count, capacity, width),
+        compiler_params=pltpu.CompilerParams(
+            collective_id=1, has_side_effects=True, vmem_limit_bytes=14 * 1024 * 1024
+        ),
+    )(slots, noise)
+
+
+def targets_kernel(rows_ref, weights_ref, out_hbm, made, sem):
+    members = rows_ref.shape[0]
+    part_width = 2 * LANES
+
+    def out_copy(q):
+        start = pl.multiple_of(q * part_width, part_width)
+        return pltpu.make_async_copy(
+            made.at[q], out_hbm.at[:, pl.ds(start, part_width)], sem.at[q]
+        )
+
+    @pl.loop(0, members)
+    def _(q):
+        panel = jnp.concatenate([rows_ref[q, 0], rows_ref[q, 1]], axis=1)
+        made[q] = jnp.dot(weights_ref[...], panel, preferred_element_type=jnp.float32)
+        out_copy(q).start()
+
+    @pl.loop(0, members)
+    def _(q):
+        out_copy(q).wait()
 
 
 def multiply(rows, weights):
-    members, _, capacity, _ = rows.shape
+    members = rows.shape[0]
     noise_count = weights.shape[0]
     width = members * 2 * LANES
-    vmem = pl.BlockSpec(memory_space=pltpu.VMEM)
     return pl.pallas_call(
         targets_kernel,
-        out_shape=jax.ShapeDtypeStruct((noise_count, width), jnp.float32),
-        grid=(members,),
-        in_specs=[vmem, vmem],
-        out_specs=pl.BlockSpec((noise_count, 2 * LANES), lambda q: (0, q)),
-        compiler_params=pltpu.CompilerParams(vmem_limit_bytes=24 * 1024 * 1024),
+        out_shape=pltpu.HBM((noise_count, width), jnp.float32),
+        in_specs=[IN_VMEM, IN_VMEM],
+        out_specs=IN_HBM,
+        scratch_shapes=[
+            pltpu.VMEM((members, noise_count, 2 * LANES), jnp.float32),
+            pltpu.SemaphoreType.DMA((members,)),
+        ],
+        compiler_params=pltpu.CompilerParams(vmem_limit_bytes=12 * 1024 * 1024),
     )(rows, weights)
 
 
 def body(loader_rows, dest_bucket, dest_slot, noise):
-    slots, counts = route(dest_bucket, loader_rows)
-
-    def all_slots(slots, counts, noise):
-        return multiply(*pair(slots, counts, noise, slots.shape[1] * ROWS_DEV, 2))
-
-    def live_first(slots, counts, noise):
-        return multiply(*pair(slots, counts, noise, FAST_ROWS, 0))
-
-    return lax.cond(jnp.all(counts <= FAST_ROWS), live_first, all_slots, slots, counts, noise)
+    rows, weights, slots, counts = pair_live_rows(dest_bucket, loader_rows, noise)
+
+    targets = multiply(rows, weights)
+
+    def with_all_slots(state):
+        return jnp.zeros((), jnp.bool_), multiply(*pair_all_slots(slots, noise))
+
+    overfull = jnp.any(counts > FAST_ROWS)
+    return lax.while_loop(lambda state: state[0], with_all_slots, (overfull, targets))[1]
 
 
 def solution(mesh):

time: 115 us -> 111 us (0.965)
  local copies, waits for them, and re-layouts: 3.89 us -> 0 us
    unnamed x6 -> x0, local copies, waits for them, and re-layouts: 3.89 us -> none
    pallas_call x3 -> x2, Pallas kernels: 109 us -> 109 us  [the longest x1 103 us: pair_live_rows(): pl.pallas_call(functools.partial(live_rows_kernel, width, FAST_ROWS), out...]
where the time goes in v4:
time: 111 us
  Pallas kernels  109 us (98%)
    pallas_call x1, Pallas kernels, pair_live_rows(): pl.pallas_call(functools.partial(live_rows_kernel, width, FAST_ROWS), out...  103 us
    pallas_call x1, Pallas kernels, multiply(): pl.pallas_call(targets_kernel, out_shape=pltpu.HBM((noise_count, width),...  6.37 us

profile of v4, /device:TPU:0, one launch (start us, length us, event | category | flops | bytes accessed | tf_op | source)
XLA Modules:
  0.0 111.0 jit_solution(9633653335307651650)
XLA Ops:
  0.0 103.0 %shard_map.37 = (bf16[16,2,1152,128]{3,2,1,0:T(8,128)(2,1)S(1)}, bf16[256,1152]{1,0:T(8,128)(2,1)S(1)}, bf16[2,16,128,128]{3,2,1,0:T(8,128)(2,1)S(1)}, f32[8,128]{1,0:T(8,128)S(1)}) custom-call(s32[1,64]{1,0:T(1,128)} %bitcast.1, f32[64,4096]{1,0:T(8,128)} %loaded_hbm.1, f32[256,4096]{1,0:T(8,128)} %noise_hbm.1), custom_call_target="tpu_custom_call" | custom-call | tf_op jit(solution)/shard_map/pallas_call | solution.py:539
  103.0 6.4 %shard_map.38 = f32[256,4096]{1,0:T(8,128)} custom-call(bf16[16,2,1152,128]{3,2,1,0:T(8,128)(2,1)S(1)} %get-tuple-element.32.rows_ref, bf16[256,1152]{1,0:T(8,128)(2,1)S(1)} %get-tuple-element.33.weights_ref), custom_call_target="tpu_custom_call" | custom-call | tf_op jit(solution)/shard_map/pallas_call | solution.py:618
  109.4 0.6 compare_reduce_fusion
  110.0 0.8 while.9

commit v5 on v4

--- a/solution.py
+++ b/solution.py
@@ -12,7 +12,7 @@
 ITERS = 4
 SIDE = 4
 BUCKETS = 8
-FAST_ROWS = 1120
+FAST_ROWS = 1104
 LANES = 128
 EMPTY = 16384.0
 MESH = pl.DeviceIdType.MESH
@@ -296,12 +296,11 @@
     rows,
     weights,
     slots_ref,
-    count_ref,
+    over_ref,
     dest_ref,
     loaded_ref,
     packed,
     landed,
-    tally,
     tally_bucket,
     tally_member,
     load_sem,
@@ -352,7 +351,9 @@
     pick = pick.astype(jnp.float32)
     fill = EMPTY * (1.0 - jnp.sum(pick, axis=1, keepdims=True))
     pick = pick.astype(jnp.bfloat16)
-    tally[0] = jnp.broadcast_to(jnp.sum(hits, axis=1, keepdims=True), tally.shape[1:])
+    tally_bucket[my_bucket] = jnp.broadcast_to(
+        jnp.sum(hits, axis=1, keepdims=True), (groups, LANES)
+    )
     load_copy.wait()
 
     def pack(k):
@@ -390,10 +391,10 @@
         copy.start()
         return copy
 
-    def tell(stage, k, target, axis, peer):
+    def tell(stage, k, source, target, axis, peer):
         copy = pltpu.make_async_remote_copy(
-            src_ref=tally.at[stage],
-            dst_ref=target.at[k],
+            src_ref=source,
+            dst_ref=target,
             send_sem=tally_send.at[stage, k],
             recv_sem=tally_recv.at[stage, k],
             device_id={axis: peer},
@@ -405,7 +406,10 @@
     for k in range(members):
         pack(k)
     pl.semaphore_wait(barrier, groups + members - 2)
-    bucket_tally = [tell(0, k, tally_bucket, "bucket", bucket_peers[k]) for k in range(1, groups)]
+    my_tally = tally_bucket.at[my_bucket]
+    bucket_tally = [
+        tell(0, k, my_tally, my_tally, "bucket", bucket_peers[k]) for k in range(1, groups)
+    ]
     first_bucket, first_member = [], []
     for k in range(1, members):
         if k < groups:
@@ -414,6 +418,17 @@
     landed[0, :, block_of(my_bucket), :] = packed[0, :, block_of(my_bucket), :]
     landed[1, me] = packed[1, 0]
 
+    for copy in bucket_tally:
+        copy.wait_recv()
+    total = jnp.zeros((groups, LANES), jnp.float32)
+    for b in range(groups):
+        tally_member[me, b : b + 1, :] = tally_bucket[b, pl.ds(my_bucket, 1), :]
+        total += tally_bucket[b]
+    tally_member[me, groups:, :] = total
+    my_tallies = tally_member.at[me]
+    member_tally = [
+        tell(1, k, my_tallies, my_tallies, "member", member_peers[k]) for k in range(1, members)
+    ]
     noise_norm = round_noise(noise_copies, noise_wide, noise_rows)
     if sent < capacity:
         blank = jnp.zeros((capacity - sent, LANES), jnp.bfloat16)
@@ -431,15 +446,21 @@
         copy.wait_recv()
     second_bucket = [to_bucket(1, k, landed.at[1], slots_ref.at[1]) for k in range(1, groups)]
     slots_ref[1, :, block_of(my_bucket), :] = landed[1, :, block_of(my_bucket), :]
-    total = tally[0]
-    for k in range(1, groups):
-        bucket_tally[k - 1].wait_recv()
-        total += tally_bucket[k]
-    tally[1] = total
-    member_tally = [tell(1, k, tally_member, "member", member_peers[k]) for k in range(1, members)]
-
     def find_positions():
-        alive = marked_live(slots_ref)
+        for copy in member_tally:
+            copy.wait_recv()
+        lane = lax.broadcasted_iota(jnp.int32, (groups, LANES), 1)
+        loader = lax.broadcasted_iota(jnp.int32, (groups, LANES), 0)
+        of_loader = (lane // block == loader).astype(jnp.float32)
+        filled = jnp.concatenate(
+            [
+                jnp.sum(of_loader * tally_member[m, :groups, :], axis=0, keepdims=True)
+                for m in range(members)
+            ],
+            axis=0,
+        )
+        slot = lax.broadcasted_iota(jnp.int32, (members, LANES), 1) % block
+        alive = (slot.astype(jnp.float32) < filled).astype(jnp.float32)
         before = (
             lax.broadcasted_iota(jnp.int32, (LANES, LANES), 0)
             <= lax.broadcasted_iota(jnp.int32, (LANES, LANES), 1)
@@ -459,37 +480,32 @@
         place += lax.broadcasted_iota(jnp.int32, (tiles, LANES), 1)
         live[...] = (place.astype(jnp.float32) < held).astype(jnp.float32)
 
-    step = capacity // 3
+    find_positions()
+    step = capacity // 9
+
+    for start in range(0, capacity, step):
+        target = lax.broadcasted_iota(jnp.int32, (step, LANES), 0) + start
+        target = target.astype(jnp.float32)
+        for t in range(start // LANES, members):
+            choose[start : start + step, t * LANES : (t + 1) * LANES] = (
+                target == position[t : t + 1, :]
+            ).astype(jnp.bfloat16)
 
     def prepare(part):
         for copy in second_bucket if part else second_member:
             copy.wait_recv()
-        if part == 0:
-            find_positions()
-
-        @pl.loop(0, 3)
-        def _(c):
-            start = pl.multiple_of(c * step, LANES)
-            span = pl.ds(start, step)
-            if part == 0:
-                target = lax.broadcasted_iota(jnp.int32, (step, LANES), 0) + start
-                target = target.astype(jnp.float32)
-                for t in range(members):
-                    choose[span, t * LANES : (t + 1) * LANES] = (
-                        target == position[t : t + 1, :]
-                    ).astype(jnp.bfloat16)
-            rows[me, part, span, :] = jnp.dot(
-                choose[span, :],
-                slots_ref[part].reshape(members * ROWS_DEV, LANES),
+        slots = slots_ref[part].reshape(members * ROWS_DEV, LANES)
+        for start in range(0, capacity, step):
+            rows[me, part, start : start + step, :] = jnp.dot(
+                choose[start : start + step, start:], slots[start:],
                 preferred_element_type=jnp.float32,
             ).astype(jnp.bfloat16)
 
     def finish_count():
-        total = tally[1]
-        for k in range(1, members):
-            member_tally[k - 1].wait_recv()
-            total += tally_member[k]
-        count_ref[...] = total
+        total = tally_member[0, groups:, :]
+        for m in range(1, members):
+            total += tally_member[m, groups:, :]
+        over_ref[0, 0] = (jnp.max(total) > sent).astype(jnp.int32)
 
     solve(width, sent, True, prepare, finish_count, lambda: noise_norm, rows, weights, scratch)
     for copy in (
@@ -542,18 +558,17 @@
             jax.ShapeDtypeStruct((members, 2, capacity, LANES), jnp.bfloat16),
             jax.ShapeDtypeStruct((noise_count, capacity), jnp.bfloat16),
             jax.ShapeDtypeStruct((2, members, ROWS_DEV, LANES), jnp.bfloat16),
-            jax.ShapeDtypeStruct((BUCKETS, LANES), jnp.float32),
+            jax.ShapeDtypeStruct((1, 1), jnp.int32),
         ),
         in_specs=[IN_HBM, IN_HBM, IN_HBM],
-        out_specs=(IN_VMEM, IN_VMEM, IN_VMEM, IN_VMEM),
+        out_specs=(IN_VMEM, IN_VMEM, IN_VMEM, pl.BlockSpec(memory_space=pltpu.SMEM)),
         scratch_shapes=[
             pltpu.VMEM((1, loaded), jnp.int32),
             pltpu.VMEM((loaded, width), jnp.float32),
             pltpu.VMEM((2, members, ROWS_DEV, LANES), jnp.bfloat16),
             pltpu.VMEM((2, members, ROWS_DEV, LANES), jnp.bfloat16),
-            pltpu.VMEM((2, BUCKETS, LANES), jnp.float32),
             pltpu.VMEM((BUCKETS, BUCKETS, LANES), jnp.float32),
-            pltpu.VMEM((members, BUCKETS, LANES), jnp.float32),
+            pltpu.VMEM((members, 2 * BUCKETS, LANES), jnp.float32),
             dma((2,)),
             dma((2, BUCKETS)),
             dma((2, BUCKETS)),
@@ -566,7 +581,7 @@
             *solve_scratch(noise_count, capacity, width),
         ],
         compiler_params=pltpu.CompilerParams(
-            collective_id=0, has_side_effects=True, vmem_limit_bytes=20 * 1024 * 1024
+            collective_id=0, has_side_effects=True, vmem_limit_bytes=24 * 1024 * 1024
         ),
     )(*[in_hbm(array) for array in (dest_bucket.reshape(1, -1), loader_rows, noise)])
 
@@ -600,7 +615,7 @@
             made.at[q], out_hbm.at[:, pl.ds(start, part_width)], sem.at[q]
         )
 
-    @pl.loop(0, members)
+    @pl.loop(0, members, unroll=16)
     def _(q):
         panel = jnp.concatenate([rows_ref[q, 0], rows_ref[q, 1]], axis=1)
         made[q] = jnp.dot(weights_ref[...], panel, preferred_element_type=jnp.float32)
@@ -629,15 +644,13 @@
 
 
 def body(loader_rows, dest_bucket, dest_slot, noise):
-    rows, weights, slots, counts = pair_live_rows(dest_bucket, loader_rows, noise)
-
+    rows, weights, slots, over = pair_live_rows(dest_bucket, loader_rows, noise)
     targets = multiply(rows, weights)
 
     def with_all_slots(state):
-        return jnp.zeros((), jnp.bool_), multiply(*pair_all_slots(slots, noise))
-
-    overfull = jnp.any(counts > FAST_ROWS)
-    return lax.while_loop(lambda state: state[0], with_all_slots, (overfull, targets))[1]
+        return jnp.zeros((), jnp.int32), multiply(*pair_all_slots(slots, noise))
+
+    return lax.while_loop(lambda state: state[0] > 0, with_all_slots, (over[0, 0], targets))[1]
 
 
 def solution(mesh):

time: 111 us -> 106 us (0.955)
  Pallas kernels: 109 us -> 106 us
    pallas_call x1, Pallas kernels: 6.37 us -> 3.88 us  [multiply(): pl.pallas_call(targets_kernel, out_shape=pltpu.HBM((noise_count, width),...]
    pallas_call x1, Pallas kernels: 103 us -> 102 us  [pair_live_rows(): pl.pallas_call(functools.partial(live_rows_kernel, width, FAST_ROWS), out...]
where the time goes in v5:
time: 106 us
  Pallas kernels  106 us (100%)
    pallas_call x1, Pallas kernels, pair_live_rows(): pl.pallas_call(functools.partial(live_rows_kernel, width, FAST_ROWS), out...  102 us
    pallas_call x1, Pallas kernels, multiply(): pl.pallas_call(targets_kernel, out_shape=pltpu.HBM((noise_count, width),...  3.88 us

profile of v5, /device:TPU:0, one launch (start us, length us, event | category | flops | bytes accessed | tf_op | source)
XLA Modules:
  0.0 106.4 jit_solution(1656499917698451678)
XLA Ops:
  0.0 101.7 %shard_map.37 = (bf16[16,2,1152,128]{3,2,1,0:T(8,128)(2,1)S(1)}, bf16[256,1152]{1,0:T(8,128)(2,1)S(1)}, bf16[2,16,128,128]{3,2,1,0:T(8,128)(2,1)S(1)}, s32[1,1]{1,0:T(1,128)}) custom-call(s32[1,64]{1,0:T(1,128)} %bitcast.2, f32[64,4096]{1,0:T(8,128)} %loaded_hbm.1, f32[256,4096]{1,0:T(8,128)} %noise_hbm.1), custom_call_target="tpu_custom_call" | custom-call | tf_op jit(solution)/shard_map/pallas_call | solution.py:555
  101.7 3.9 %shard_map.38 = f32[256,4096]{1,0:T(8,128)} custom-call(bf16[16,2,1152,128]{3,2,1,0:T(8,128)(2,1)S(1)} %get-tuple-element.32.rows_ref, bf16[256,1152]{1,0:T(8,128)(2,1)S(1)} %get-tuple-element.33.weights_ref), custom_call_target="tpu_custom_call" | custom-call | tf_op jit(solution)/shard_map/pallas_call | solution.py:633
  105.6 0.6 while.9

commit v6 on v5

--- a/solution.py
+++ b/solution.py
@@ -17,6 +17,13 @@
 EMPTY = 16384.0
 MESH = pl.DeviceIdType.MESH
 CONTRACT_LAST = (((1,), (1,)), ((), ()))
+
+
+def hops(k):
+    return sum(min(step, SIDE - step) for step in (k // SIDE, k % SIDE))
+
+
+FAR_FIRST = sorted(range(1, SIDE * SIDE), key=lambda k: -hops(k))
 
 
 def solve(width, sent, eager, prepare, extra, noise_norm_of, rows, weights, scratch):
@@ -183,13 +190,13 @@
             total = jnp.sum(jnp.exp(scores - peak), axis=0, keepdims=True)
             lse_out[it, t : t + 1, :] = peak + jnp.log(total)
         lse_copies = []
-        for k in range(1, members):
+        for k in FAR_FIRST:
             copy = pltpu.make_async_remote_copy(
                 src_ref=lse_out.at[it],
                 dst_ref=lse_in.at[it, k],
                 send_sem=lse_send.at[it, k],
                 recv_sem=lse_recv.at[it, k],
-                device_id={"member": (me + k) % members},
+                device_id={"member": member_at(0, k % SIDE, k // SIDE)},
                 device_id_type=MESH,
             )
             copy.start()
@@ -325,7 +332,10 @@
     block = ROWS_DEV // groups
     my_bucket, me = lax.axis_index("bucket"), lax.axis_index("member")
     bucket_peers = [(my_bucket + k) % groups for k in range(groups)]
-    member_peers = [(me + k) % members for k in range(members)]
+    member_peers = [
+        ((me // SIDE + k // SIDE) % SIDE) * SIDE + (me % SIDE + k % SIDE) % SIDE
+        for k in range(members)
+    ]
 
     dest_copy = pltpu.make_async_copy(dest_hbm, dest_ref, load_sem.at[0])
     dest_copy.start()
@@ -405,16 +415,33 @@
 
     for k in range(members):
         pack(k)
+    first_bucket, second_member = {}, []
+
+    def send_quarter(c):
+        quarter = pl.ds(SIDE * c, SIDE)
+        for k in range(1, groups):
+            first_bucket[c, k] = to_bucket(
+                c, k, packed.at[0, quarter], landed.at[0, quarter]
+            )
+
+    def pass_quarter(c):
+        for k in range(1, groups):
+            first_bucket[c, k].wait_recv()
+        for k in FAR_FIRST:
+            if k // SIDE == c:
+                second_member.append(to_member(1, k, landed.at[0, k], slots_ref.at[0, me]))
+        if c == 0:
+            slots_ref[0, me] = landed[0, 0]
+
+    order = (2, 1, 3, 0)
     pl.semaphore_wait(barrier, groups + members - 2)
     my_tally = tally_bucket.at[my_bucket]
     bucket_tally = [
         tell(0, k, my_tally, my_tally, "bucket", bucket_peers[k]) for k in range(1, groups)
     ]
-    first_bucket, first_member = [], []
-    for k in range(1, members):
-        if k < groups:
-            first_bucket.append(to_bucket(0, k, packed.at[0], landed.at[0]))
-        first_member.append(to_member(0, k, packed.at[1, k], landed.at[1, me]))
+    send_quarter(order[0])
+    first_member = [to_member(0, k, packed.at[1, k], landed.at[1, me]) for k in FAR_FIRST]
+    send_quarter(order[1])
     landed[0, :, block_of(my_bucket), :] = packed[0, :, block_of(my_bucket), :]
     landed[1, me] = packed[1, 0]
 
@@ -427,8 +454,20 @@
     tally_member[me, groups:, :] = total
     my_tallies = tally_member.at[me]
     member_tally = [
-        tell(1, k, my_tallies, my_tallies, "member", member_peers[k]) for k in range(1, members)
+        tell(1, k, my_tallies, my_tallies, "member", member_peers[k]) for k in FAR_FIRST
     ]
+    for i in range(2):
+        for k in range(1, groups):
+            first_bucket[order[i], k].wait_send()
+        send_quarter(order[i + 2])
+        pass_quarter(order[i])
+    pass_quarter(order[2])
+    pass_quarter(order[3])
+    for copy in first_member:
+        copy.wait_recv()
+    second_bucket = [to_bucket(4, k, landed.at[1], slots_ref.at[1]) for k in range(1, groups)]
+    slots_ref[1, :, block_of(my_bucket), :] = landed[1, :, block_of(my_bucket), :]
+
     noise_norm = round_noise(noise_copies, noise_wide, noise_rows)
     if sent < capacity:
         blank = jnp.zeros((capacity - sent, LANES), jnp.bfloat16)
@@ -436,16 +475,6 @@
             for part in range(2):
                 rows[q, part, sent:capacity, :] = blank
 
-    for copy in first_bucket:
-        copy.wait_recv()
-    second_member = [
-        to_member(1, k, landed.at[0, k], slots_ref.at[0, me]) for k in range(1, members)
-    ]
-    slots_ref[0, me] = landed[0, 0]
-    for copy in first_member:
-        copy.wait_recv()
-    second_bucket = [to_bucket(1, k, landed.at[1], slots_ref.at[1]) for k in range(1, groups)]
-    slots_ref[1, :, block_of(my_bucket), :] = landed[1, :, block_of(my_bucket), :]
     def find_positions():
         for copy in member_tally:
             copy.wait_recv()
@@ -509,7 +538,8 @@
 
     solve(width, sent, True, prepare, finish_count, lambda: noise_norm, rows, weights, scratch)
     for copy in (
-        first_bucket + first_member + second_member + second_bucket + bucket_tally + member_tally
+        [first_bucket[c, k] for c in order[2:] for k in range(1, groups)]
+        + first_member + second_member + second_bucket + bucket_tally + member_tally
     ):
         copy.wait_send()
 
@@ -570,8 +600,8 @@
             pltpu.VMEM((BUCKETS, BUCKETS, LANES), jnp.float32),
             pltpu.VMEM((members, 2 * BUCKETS, LANES), jnp.float32),
             dma((2,)),
-            dma((2, BUCKETS)),
-            dma((2, BUCKETS)),
+            dma((5, BUCKETS)),
+            dma((5, BUCKETS)),
             dma((2, members)),
             dma((2, members)),
             dma((2, members)),

time: 106 us -> 103 us (0.972)
  Pallas kernels: 106 us -> 102 us
    pallas_call x1, Pallas kernels: 102 us -> 98.3 us  [pair_live_rows(): pl.pallas_call(functools.partial(live_rows_kernel, width, FAST_ROWS), out...]
where the time goes in v6:
time: 103 us
  Pallas kernels  102 us (99%)
    pallas_call x1, Pallas kernels, pair_live_rows(): pl.pallas_call(functools.partial(live_rows_kernel, width, FAST_ROWS), out...  98.3 us
    pallas_call x1, Pallas kernels, multiply(): pl.pallas_call(targets_kernel, out_shape=pltpu.HBM((noise_count, width),...  3.88 us

profile of v6, /device:TPU:0, one launch (start us, length us, event | category | flops | bytes accessed | tf_op | source)
XLA Modules:
  0.0 103.0 jit_solution(18273197032449116087)
XLA Ops:
  0.0 98.3 %shard_map.37 = (bf16[16,2,1152,128]{3,2,1,0:T(8,128)(2,1)S(1)}, bf16[256,1152]{1,0:T(8,128)(2,1)S(1)}, bf16[2,16,128,128]{3,2,1,0:T(8,128)(2,1)S(1)}, s32[1,1]{1,0:T(1,128)}) custom-call(s32[1,64]{1,0:T(1,128)} %bitcast.2, f32[64,4096]{1,0:T(8,128)} %loaded_hbm.1, f32[256,4096]{1,0:T(8,128)} %noise_hbm.1), custom_call_target="tpu_custom_call" | custom-call | tf_op jit(solution)/shard_map/pallas_call | solution.py:585
  98.3 3.9 %shard_map.38 = f32[256,4096]{1,0:T(8,128)} custom-call(bf16[16,2,1152,128]{3,2,1,0:T(8,128)(2,1)S(1)} %get-tuple-element.32.rows_ref, bf16[256,1152]{1,0:T(8,128)(2,1)S(1)} %get-tuple-element.33.weights_ref), custom_call_target="tpu_custom_call" | custom-call | tf_op jit(solution)/shard_map/pallas_call | solution.py:663
  102.2 0.6 while.9

commit v7 on v6

--- a/solution.py
+++ b/solution.py
@@ -133,14 +133,14 @@
         for d in range(2):
             arrive(("g1", part, 0, d))
             second_forward(part, 0, d)
-    for step in ways:
-        add_slice(member_at(0, step, 0))
-        add_slice(member_at(0, 0, step))
     for d in range(2):
         for part in range(2):
             arrive(("f2", part, d))
             for e in range(2):
                 second_hop(part, 3 + d, e)
+    for step in ways:
+        add_slice(member_at(0, step, 0))
+        add_slice(member_at(0, 0, step))
     for u in (1, 2):
         for part in range(2):
             for d in range(2):
@@ -176,16 +176,15 @@
     if not eager:
         pl.loop(0, members)(add_panel)
 
-    for t in range(tiles):
-        lanes = slice(t * LANES, (t + 1) * LANES)
-        cost[:, lanes] = (2.0 * cost[:, lanes] - row_norm[0:1, lanes] - noise_norm) * scale
-
-    col_shift[...] = jnp.zeros_like(col_shift)
     row_chunk = 32
     for it in range(ITERS):
         for t in range(tiles):
             lanes = slice(t * LANES, (t + 1) * LANES)
-            scores = cost[:, lanes] + col_shift[...]
+            if it == 0:
+                scores = (2.0 * cost[:, lanes] - row_norm[0:1, lanes] - noise_norm) * scale
+                cost[:, lanes] = scores
+            else:
+                scores = cost[:, lanes] + col_shift[...]
             peak = jnp.max(scores, axis=0, keepdims=True)
             total = jnp.sum(jnp.exp(scores - peak), axis=0, keepdims=True)
             lse_out[it, t : t + 1, :] = peak + jnp.log(total)
@@ -337,17 +336,19 @@
         for k in range(members)
     ]
 
+    barrier = pltpu.get_barrier_semaphore()
+    for k in FAR_FIRST:
+        pl.semaphore_signal(
+            barrier, inc=1, device_id={"member": member_peers[k]}, device_id_type=MESH
+        )
+    for peer in bucket_peers[1:]:
+        pl.semaphore_signal(barrier, inc=1, device_id={"bucket": peer}, device_id_type=MESH)
+
     dest_copy = pltpu.make_async_copy(dest_hbm, dest_ref, load_sem.at[0])
     dest_copy.start()
     load_copy = pltpu.make_async_copy(loaded_hbm, loaded_ref, load_sem.at[1])
     load_copy.start()
     noise_copies = start_noise(noise_hbm, noise_wide, noise_sem)
-    barrier = pltpu.get_barrier_semaphore()
-    for peer in bucket_peers[1:]:
-        pl.semaphore_signal(barrier, inc=1, device_id={"bucket": peer}, device_id_type=MESH)
-    for peer in member_peers[1:]:
-        pl.semaphore_signal(barrier, inc=1, device_id={"member": peer}, device_id_type=MESH)
-
     dest_copy.wait()
     dest = dest_ref[...]
     hits = (lax.broadcasted_iota(jnp.int32, (groups, loaded), 0) == dest).astype(jnp.float32)

time: 103 us -> 103 us (level)
  no operation moved by 1% of the time
where the time goes in v7:
time: 103 us
  Pallas kernels  102 us (99%)
    pallas_call x1, Pallas kernels, pair_live_rows(): pl.pallas_call(functools.partial(live_rows_kernel, width, FAST_ROWS), out...  98.2 us
    pallas_call x1, Pallas kernels, multiply(): pl.pallas_call(targets_kernel, out_shape=pltpu.HBM((noise_count, width),...  3.88 us

profile of v7, /device:TPU:0, one launch (start us, length us, event | category | flops | bytes accessed | tf_op | source)
XLA Modules:
  0.0 102.9 jit_solution(4526756311135624567)
XLA Ops:
  0.0 98.2 %shard_map.37 = (bf16[16,2,1152,128]{3,2,1,0:T(8,128)(2,1)S(1)}, bf16[256,1152]{1,0:T(8,128)(2,1)S(1)}, bf16[2,16,128,128]{3,2,1,0:T(8,128)(2,1)S(1)}, s32[1,1]{1,0:T(1,128)}) custom-call(s32[1,64]{1,0:T(1,128)} %bitcast.2, f32[64,4096]{1,0:T(8,128)} %loaded_hbm.1, f32[256,4096]{1,0:T(8,128)} %noise_hbm.1), custom_call_target="tpu_custom_call" | custom-call | tf_op jit(solution)/shard_map/pallas_call | solution.py:586
  98.2 3.9 %shard_map.38 = f32[256,4096]{1,0:T(8,128)} custom-call(bf16[16,2,1152,128]{3,2,1,0:T(8,128)(2,1)S(1)} %get-tuple-element.32.rows_ref, bf16[256,1152]{1,0:T(8,128)(2,1)S(1)} %get-tuple-element.33.weights_ref), custom_call_target="tpu_custom_call" | custom-call | tf_op jit(solution)/shard_map/pallas_call | solution.py:664
  102.1 0.6 while.9
